TPU v7x, 256 devices: a whole 4x4x8 slice. The times are simulated.
256 devices in a mesh: fsdp: 16 (over y, z_hi), seq: 16 (over x, z_lo, core).
Axes of the slice: x: 4, y: 4, z: 8 (z_hi: 4, z_lo: 2; z = z_hi * 2 + z_lo), core: 2. Of those that a mesh axis runs over, the one named last changes fastest.
Arguments:
- hidden: bfloat16 [16, 2048, 5120], P('fsdp', 'seq'), may hold values from -6 to 6
- queries: bfloat16 [16, 2048, 4096], P('fsdp', 'seq'), may hold values from -400 to 400
- key_value_weight: bfloat16 [5120, 2048], P('fsdp'), may hold values from -0.078125 to 0.078125
- doc_lengths: int32 [16, 16], P('fsdp'), may hold values from 1 to 1024, 2048 in all within a row
- resp_lengths: int32 [16, 16], P('fsdp'), may hold values from 1 to 128
Outputs:
- attended: bfloat16 [16, 2048, 4096], P('fsdp', 'seq')
- pooled: float32 [16, 16, 4096], P('fsdp', None, 'seq')
Inputs may be any that keep to these rules, and one draw needn't show every extreme that they name: `doc_lengths`: each row holds the lengths of the documents of one packed sequence in order; they sum to 2048 and the longest is exactly 1024.
All inputs are finite; a program needn't handle non-finite values.
Results may differ from a plain program's by a relative error of at most 0.011.
Values may be sent and summed in bfloat16 or wider, within the bound.
No kernel may reach another device: no remote copies, remote signals or barrier semaphores. Data moves between devices by JAX's collectives and lax.ppermute only.
A program may use at most 128 MiB of HBM per device.

v0:
```python
import functools

import jax
import jax.numpy as jnp
from jax import lax
from jax.experimental import pallas as pl
from jax.experimental.pallas import tpu as pltpu
from jax.sharding import PartitionSpec as P


HEAD = 128
TOK = 128
WIDTH = 5120
ROWS = 320
HALF = 160
COLS = 512
OCOLS = 1024
DOCS = 16
ROPE_BASE = 1000000.0
NEG = -1e30
LOG2E = 1.4426950408889634
BF = jnp.bfloat16
F32 = jnp.float32
MIB = 1 << 20
CHUNK = 256


def shift(v, axis, d):
    n = lax.axis_size(axis)
    return lax.ppermute(v, axis, [(i, (i + d) % n) for i in range(n)])


def proj_kernel(n, *refs):
    idx, hs, refs = refs[0], refs[1 : 1 + n], refs[1 + n :]
    sets, refs = (refs[:8], refs[8:16]), refs[16:]
    cos_ref, sin_ref, out_ref, wbuf, acc = refs
    core, zh, my_y = idx[0], idx[1], idx[2]
    span = 4 * ROWS
    for d in range(4):
        for m, c in enumerate((core, 1 - core)):
            for r, turn in enumerate((0, 3, 1)):
                wbuf[d, lax.rem(zh + turn, 4), c] = sets[m][d][r]
            wbuf[d, lax.rem(zh + 2, 4), c] = sets[m][4 + d][...]
        start = pl.multiple_of(lax.rem(my_y + 4 - d, 4) * span, HEAD)
        h = jnp.concatenate([ref[:, pl.ds(start, span)] for ref in hs], axis=0)
        p = jnp.dot(h, wbuf[d].reshape(span, COLS), preferred_element_type=F32)
        if d == 0:
            acc[...] = p
        elif d < 3:
            acc[...] = acc[...] + p
    p = acc[...] + p
    cos, sin = cos_ref[...], sin_ref[...]
    for k in range(4):
        v = p[:, k * HEAD : (k + 1) * HEAD]
        if k < 2:
            v = v * cos + pltpu.roll(v, 64, 1) * sin
        out_ref[:, k * HEAD : (k + 1) * HEAD] = v.astype(BF)


def project(idx, pieces, weights, cos, sin):
    row = sum(h.shape[0] for h in pieces)
    vm = pl.BlockSpec(memory_space=pltpu.VMEM)
    return pl.pallas_call(
        functools.partial(proj_kernel, len(pieces)),
        out_shape=jax.ShapeDtypeStruct((row, COLS), BF),
        in_specs=[pl.BlockSpec(memory_space=pltpu.SMEM)] + [vm] * (len(pieces) + 18),
        out_specs=vm,
        scratch_shapes=[
            pltpu.VMEM((4, 4, 2, HALF, COLS), BF),
            pltpu.VMEM((row, COLS), F32),
        ],
        compiler_params=pltpu.CompilerParams(vmem_limit_bytes=21 * MIB),
        cost_estimate=pl.CostEstimate(
            flops=2 * row * WIDTH * COLS, bytes_accessed=18 * MIB, transcendentals=0
        ),
        name="project",
    )(idx, *pieces, *weights, cos, sin)


def attn_kernel(js, *refs):
    n = len(js)
    idx, qs_ref, mem_ref, prev_ref = refs[:4]
    q_refs, kv_in, refs = refs[4 : 4 + n], refs[4 + n : 12 + n], refs[12 + n :]
    o_refs, refs = refs[:n], refs[n:]
    pool_ref, kvbuf, sbuf, mx, ls, acc = refs
    for g in range(4):
        for j in range(4):
            to = pl.ds(pl.multiple_of(idx[g * 4 + j] * TOK, TOK), TOK)
            row = j % 3 * TOK
            kvbuf[to, :] = kv_in[2 * g + j // 3][row : row + TOK, :]
    kvbuf[pl.ds(16 * TOK, TOK), :] = jnp.zeros((TOK, COLS), BF)
    row = lax.broadcasted_iota(jnp.int32, (TOK, CHUNK), 0)
    lane = lax.broadcasted_iota(jnp.int32, (TOK, CHUNK), 1)
    factor = HEAD ** (-0.5) * LOG2E
    total = jnp.zeros((DOCS, OCOLS), F32)
    for t, j in enumerate(js):
        lo, hi = idx[16 + j], idx[20 + j]
        n_chunks = (hi - lo) // 2 + 1
        first = jnp.concatenate([qs_ref[j], qs_ref[j]], axis=1) - lane
        last = row - lane + hi * TOK
        mx[...] = jnp.full((2, 4 * TOK, TOK), NEG, F32)
        ls[...] = jnp.zeros((2, 4 * TOK, TOK), F32)
        acc[...] = jnp.zeros((2, 4 * TOK, HEAD), F32)

        def scores(i, carry, t=t, lo=lo, first=first, last=last):
            base = pl.multiple_of((lo + 2 * i) * TOK, TOK)
            mask = (first <= base) & (last >= base)
            for e in range(2):
                k = kvbuf[pl.ds(base, CHUNK), e * HEAD : (e + 1) * HEAD]
                for g in range(4):
                    h = (e * 4 + g) * HEAD
                    s = lax.dot_general(
                        q_refs[t][:, h : h + HEAD],
                        k,
                        (((1,), (1,)), ((), ())),
                        preferred_element_type=F32,
                    )
                    s = jnp.where(mask, s, NEG)
                    r = slice(g * TOK, (g + 1) * TOK)
                    sbuf[i, e, r] = s
                    m = jnp.maximum(s[:, :TOK], s[:, TOK:])
                    mx[e, r] = jnp.maximum(mx[e, r], m)
            return carry

        lax.fori_loop(0, n_chunks, scores, 0)
        for e in range(2):
            peak = jnp.max(mx[e], axis=1, keepdims=True) * factor
            mx[e] = jnp.broadcast_to(peak, (4 * TOK, TOK))

        def values(i, carry, lo=lo):
            base = pl.multiple_of((lo + 2 * i) * TOK, TOK)
            for e in range(2):
                v = kvbuf[pl.ds(base, CHUNK), 256 + e * HEAD : 256 + (e + 1) * HEAD]
                for g in range(4):
                    r = slice(g * TOK, (g + 1) * TOK)
                    peak = mx[e, r]
                    p0 = jnp.exp2(sbuf[i, e, r, :TOK] * factor - peak)
                    p1 = jnp.exp2(sbuf[i, e, r, TOK:] * factor - peak)
                    ls[e, r] = ls[e, r] + (p0 + p1)
                    p = jnp.concatenate([p0.astype(BF), p1.astype(BF)], axis=1)
                    acc[e, r] = acc[e, r] + jnp.dot(p, v, preferred_element_type=F32)
            return carry

        lax.fori_loop(0, n_chunks, values, 0)
        for e in range(2):
            den = jnp.sum(ls[e], axis=1, keepdims=True)
            o = (acc[e] / den).astype(BF)
            for g in range(4):
                h = (e * 4 + g) * HEAD
                o_refs[t][:, h : h + HEAD] = o[g * TOK : (g + 1) * TOK]
        total = total + jnp.dot(mem_ref[j], o_refs[t][...], preferred_element_type=F32)
    for zc in range(4):
        part = total[:, zc * 256 : zc * 256 + 256]
        pool_ref[zc % 2, zc // 2] = prev_ref[zc % 2, zc // 2] + part


def attend(js, idx, qs, starts, member, prev, kv):
    n = len(js)
    vm = pl.BlockSpec(memory_space=pltpu.VMEM)
    out = pl.pallas_call(
        functools.partial(attn_kernel, js),
        out_shape=[jax.ShapeDtypeStruct((TOK, OCOLS), BF)] * n
        + [jax.ShapeDtypeStruct((2, 2, DOCS, 256), F32)],
        in_specs=[pl.BlockSpec(memory_space=pltpu.SMEM)] + [vm] * (11 + n),
        out_specs=[vm] * (n + 1),
        scratch_shapes=[
            pltpu.VMEM((17 * TOK, COLS), BF),
            pltpu.VMEM((5, 2, 4 * TOK, CHUNK), F32),
            pltpu.VMEM((2, 4 * TOK, TOK), F32),
            pltpu.VMEM((2, 4 * TOK, TOK), F32),
            pltpu.VMEM((2, 4 * TOK, HEAD), F32),
        ],
        compiler_params=pltpu.CompilerParams(vmem_limit_bytes=15 * MIB),
        cost_estimate=pl.CostEstimate(
            flops=n * 2 * 2 * 1024 * 700 * 128, bytes_accessed=n * 12 * MIB, transcendentals=n * 700 * 1024
        ),
        name="attend",
    )(idx, starts, member, prev, *[qs[j] for j in js], *kv)
    return out[:n], out[n]


def assemble_kernel(idx, *refs):
    ins, out_ref = refs[:4], refs[4]
    for d in range(4):
        lo = pl.multiple_of(idx[d] * OCOLS, OCOLS)
        out_ref[0, :, pl.ds(lo, OCOLS)] = ins[d][...]


def assemble(idx, pieces):
    vm = pl.BlockSpec(memory_space=pltpu.VMEM)
    return pl.pallas_call(
        assemble_kernel,
        out_shape=jax.ShapeDtypeStruct((1, TOK, 4 * OCOLS), BF),
        in_specs=[pl.BlockSpec(memory_space=pltpu.SMEM)] + [vm] * 4,
        out_specs=vm,
        compiler_params=pltpu.CompilerParams(vmem_limit_bytes=4 * MIB),
        cost_estimate=pl.CostEstimate(flops=0, bytes_accessed=2 * MIB, transcendentals=0),
        name="assemble",
    )(idx, *pieces)


def program(hidden, queries, weight, doc_lengths, resp_lengths):
    x, zl, core = lax.axis_index("x"), lax.axis_index("zl"), lax.axis_index("c")
    zh, rest = lax.axis_index("zh"), 2 * zl + core
    h, q = hidden[0], queries[0]

    keys = lax.dynamic_slice(weight, (core * HALF, x * 256), (HALF, 256))
    vals = lax.dynamic_slice(weight, (core * HALF, OCOLS + x * 256), (HALF, 256))
    own = jnp.concatenate([keys, vals], axis=1)
    z1 = shift(own, "zh", 1)
    z3 = shift(own, "zh", -1)
    half = TOK // 2
    top, bottom = h[:half], h[half:]
    top_left = shift(top, "x", 1)
    bottom_right = shift(bottom, "x", -1)
    bottom_left = shift(bottom, "x", 1)
    top_right = shift(top, "x", -1)
    far_top = shift(top_left, "x", 1)
    far_bottom = shift(bottom_right, "x", -1)
    z2 = shift(own, "zh", 2)
    three = jnp.stack([own, z1, z3])
    mine = [three] + [None] * 3 + [z2] + [None] * 3
    for d in (1, 3, 2):
        mine[d] = shift(three, "y", d)
    for d in (1, 3, 2):
        mine[4 + d] = shift(z2, "y", d)
    weights = mine + [shift(v, "c", 1) for v in mine]

    give = lambda d: lax.dynamic_slice(q, (0, (x + d) % 4 * OCOLS), (TOK, OCOLS))
    gives = [give(d) for d in range(4)]
    q1 = shift(gives[3], "x", -1)
    q3 = shift(gives[1], "x", 1)
    q2 = shift(gives[2], "x", 2)
    qs = [gives[0], q1, q3, q2]

    lengths, wanted = doc_lengths[0], resp_lengths[0]
    ends = jnp.cumsum(lengths)
    starts = ends - lengths
    answer = jnp.minimum(wanted, lengths)
    turn = (x + jnp.array([0, 1, 3, 2], jnp.int32)) % 4
    block = turn * 4 + rest
    token = (block[:, None] * TOK + jnp.arange(TOK, dtype=jnp.int32)[None, :])[:, :, None]
    inside = (token >= starts) & (token < ends)
    begin = jnp.sum(jnp.where(inside, starts, 0), axis=2)
    member = jnp.where(inside & (token >= ends - answer), 1.0, 0.0).astype(BF)
    member = jnp.swapaxes(member, 1, 2)
    position = token[:, :, 0] - begin
    pair = jnp.arange(HEAD, dtype=jnp.int32) % (HEAD // 2)
    freq = ROPE_BASE ** (-(pair.astype(F32) * 2.0 / HEAD))
    angle = position.reshape(4 * TOK).astype(F32)[:, None] * freq
    cosine = jnp.cos(angle)
    sine = jnp.where(jnp.arange(HEAD) < HEAD // 2, -1.0, 1.0) * jnp.sin(angle)
    spread = jnp.broadcast_to(begin[:, :, None], (4, TOK, TOK))
    places = jnp.concatenate([(block ^ m) for m in range(4)])
    aidx = jnp.concatenate([places, begin[:, 0] // TOK, block]).astype(jnp.int32)
    widx = jnp.stack([core, zh, lax.axis_index("y")]).astype(jnp.int32)

    cos0, cos1 = cosine[: 3 * TOK], cosine[3 * TOK :]
    sin0, sin1 = sine[: 3 * TOK], sine[3 * TOK :]
    near = [h, top_right, bottom_right, top_left, bottom_left]
    kv_near = project(widx, near, weights, cos0, sin0)
    kv_near_z = shift(kv_near, "zl", 1)
    kv_far = project(widx, [far_top, far_bottom], weights, cos1, sin1)
    kv_far_z = shift(kv_far, "zl", 1)
    kv = []
    for near, far in ((kv_near, kv_far), (kv_near_z, kv_far_z)):
        kv.append([near, far, shift(near, "c", 1), shift(far, "c", 1)])
    kv = kv[0] + kv[1]

    pool = jnp.zeros((2, 2, DOCS, 256), F32)
    (o3,), pool = attend((3,), aidx, qs, spread, member, pool, kv)
    r3 = shift(o3, "x", 2)
    (o1, o2), pool = attend((1, 2), aidx, qs, spread, member, pool, kv)
    r2 = shift(o1, "x", 1)
    r1 = shift(o2, "x", -1)
    (o0,), pool = attend((0,), aidx, qs, spread, member, pool, kv)
    attended = assemble(turn.astype(jnp.int32), [o0, r1, r2, r3])

    pick = lambda v, i: lax.dynamic_index_in_dim(v, i, 0, keepdims=False)
    sums = pick(pool, core) + shift(pick(pool, 1 - core), "c", 1)
    sums = pick(sums, zl) + shift(pick(sums, 1 - zl), "zl", 1)
    pooled = sums / answer.astype(F32)[:, None]
    return attended, pooled[None]


def solution(mesh):
    fine = jax.sharding.Mesh(mesh.devices.reshape(4, 4, 4, 2, 2), ("y", "zh", "x", "zl", "c"))
    fsdp, seq = ("y", "zh"), ("x", "zl", "c")
    in_specs = (
        P(fsdp, seq, None),
        P(fsdp, seq, None),
        P(fsdp, None),
        P(fsdp, None),
        P(fsdp, None),
    )
    out_specs = (P(fsdp, seq, None), P(fsdp, None, seq))
    return jax.shard_map(
        program, mesh=fine, in_specs=in_specs, out_specs=out_specs, check_vma=False
    )
```

profile of v0, /device:TPU:8, one launch (start us, length us, event | category | flops | bytes accessed | tf_op | source)
XLA Modules:
  0.0 172.1 jit_solution(9254691480881451806)
XLA Ops:
  0.6 1.0 fusion.11
  1.7 7.3 %collective-permute-start.10 = (bf16[160,512]{1,0:T(8,128)(2,1)S(1)}, bf16[160,512]{1,0:T(8,128)(2,1)S(1)}, u32[]{:S(2)}, u32[]{:S(2)}) collective-permute-start(bf16[160,512]{1,0:T(8,128)(2,1)S(1)} %get-tuple-element.28), channel_id=1, source_target_pairs={{0,32},{16,48},{32,0},{48,16},{1,33},{17,49},{33,1},{49,17},{2,34}... | collective-permute-start | bytes 491528 | tf_op jit(solution)/shard_map/ppermute | solution.py:30
  9.0 1.5 collective-permute-start.5
  10.5 2.7 %collective-permute-start.6 = (bf16[160,512]{1,0:T(8,128)(2,1)S(1)}, bf16[160,512]{1,0:T(8,128)(2,1)S(1)}, u32[]{:S(2)}, u32[]{:S(2)}) collective-permute-start(bf16[160,512]{1,0:T(8,128)(2,1)S(1)} %get-tuple-element.28), channel_id=1, source_target_pairs={{0,48},{16,0},{32,16},{48,32},{1,49},{17,1},{33,17},{49,33},{2,50}... | collective-permute-start | bytes 491528 | tf_op jit(solution)/shard_map/ppermute | solution.py:30
  13.1 3.7 %collective-permute-done.10.refs_10_.refs_7_ = bf16[160,512]{1,0:T(8,128)(2,1)S(1)} collective-permute-done((bf16[160,512]{1,0:T(8,128)(2,1)S(1)}, bf16[160,512]{1,0:T(8,128)(2,1)S(1)}, u32[]{:S(2)}, u32[]{:S(2)}) %collective-permute-start.10) | collective-permute-done | bytes 163872 | tf_op jit(solution)/shard_map/ppermute | solution.py:30
  16.9 1.6 collective-permute-start.11
  18.5 2.2 %collective-permute-done.5 = bf16[160,512]{1,0:T(8,128)(2,1)S(1)} collective-permute-done((bf16[160,512]{1,0:T(8,128)(2,1)S(1)}, bf16[160,512]{1,0:T(8,128)(2,1)S(1)}, u32[]{:S(2)}, u32[]{:S(2)}) %collective-permute-start.5) | collective-permute-done | bytes 163872 | tf_op jit(solution)/shard_map/ppermute | solution.py:30
  20.6 3.7 %collective-permute-done.6 = bf16[160,512]{1,0:T(8,128)(2,1)S(1)} collective-permute-done((bf16[160,512]{1,0:T(8,128)(2,1)S(1)}, bf16[160,512]{1,0:T(8,128)(2,1)S(1)}, u32[]{:S(2)}, u32[]{:S(2)}) %collective-permute-start.6) | collective-permute-done | bytes 163872 | tf_op jit(solution)/shard_map/ppermute | solution.py:30
  24.4 1.7 collective-permute-start.7
  26.1 0.9 collective-permute-start.8
  27.0 2.4 %collective-permute-start.9 = (bf16[3,160,512]{2,1,0:T(8,128)(2,1)S(1)}, bf16[3,160,512]{2,1,0:T(8,128)(2,1)}, u32[]{:S(2)}, u32[]{:S(2)}) collective-permute-start(bf16[3,160,512]{2,1,0:T(8,128)(2,1)S(1)} %pad_maximum_fusion.refs_6_.refs_3_), channel_id=1, source_target_pairs={{0,192},{64,0},{128,64},{192,128},{1,193},{65,1},{129,65},{193,129... | collective-permute-start | bytes 1474568 | tf_op jit(solution)/shard_map/ppermute | solution.py:30
  29.6 1.5 collective-permute-start.13
  31.1 1.2 slice_bitcast_fusion
  32.6 23.2 %collective-permute-done.12.refs_12_.refs_9_ = bf16[160,512]{1,0:T(8,128)(2,1)S(1)} collective-permute-done((bf16[160,512]{1,0:T(8,128)(2,1)S(1)}, bf16[160,512]{1,0:T(8,128)(2,1)S(1)}, u32[]{:S(2)}, u32[]{:S(2)}) %collective-permute-start.12) | collective-permute-done | bytes 163872 | tf_op jit(solution)/shard_map/ppermute | solution.py:30
  55.8 1.5 collective-permute-done.13.refs_13_.refs_10_
  61.2 1.5 collective-permute-start.3
  63.3 1.7 %collective-permute-start.1 = (bf16[64,5120]{1,0:T(8,128)(2,1)}, bf16[64,5120]{1,0:T(8,128)(2,1)S(1)}, u32[]{:S(2)}, u32[]{:S(2)}) collective-permute-start(bf16[64,5120]{1,0:T(8,128)(2,1)} %get-tuple-element.22), channel_id=1, source_target_pairs={{0,12},{4,0},{8,4},{12,8},{1,13},{5,1},{9,5},{13,9},{2,14},{6,2},{... | collective-permute-start | bytes 1966088 | tf_op jit(solution)/shard_map/ppermute | solution.py:30
  65.1 1.5 collective-permute-start.2
  67.4 1.6 collective-permute-done.14.refs_14_.refs_11_
  69.9 10.4 %collective-permute-done.3.refs_4_ = bf16[64,5120]{1,0:T(8,128)(2,1)} collective-permute-done((bf16[64,5120]{1,0:T(8,128)(2,1)}, bf16[64,5120]{1,0:T(8,128)(2,1)}, u32[]{:S(2)}, u32[]{:S(2)}) %collective-permute-start.3) | collective-permute-done | bytes 655392 | tf_op jit(solution)/shard_map/ppermute | solution.py:30
  80.3 14.2 %collective-permute-done.2.refs_3_ = bf16[64,5120]{1,0:T(8,128)(2,1)} collective-permute-done((bf16[64,5120]{1,0:T(8,128)(2,1)}, bf16[64,5120]{1,0:T(8,128)(2,1)}, u32[]{:S(2)}, u32[]{:S(2)}) %collective-permute-start.2) | collective-permute-done | bytes 655392 | tf_op jit(solution)/shard_map/ppermute | solution.py:30
  95.4 1.5 collective-permute-start.22
  97.7 1.7 %collective-permute-start.23 = (bf16[64,5120]{1,0:T(8,128)(2,1)}, bf16[64,5120]{1,0:T(8,128)(2,1)}, u32[]{:S(2)}, u32[]{:S(2)}) collective-permute-start(bf16[64,5120]{1,0:T(8,128)(2,1)} %collective-permute-done.2.refs_3_), channel_id=1, source_target_pairs={{0,12},{4,0},{8,4},{12,8},{1,13},{5,1},{9,5},{13,9},{2,14},{6,2},{... | collective-permute-start | bytes 1966088 | tf_op jit(solution)/shard_map/ppermute | solution.py:30
  99.5 1.0 fusion
  102.6 2.1 %dynamic-slice_bitcast_fusion = (bf16[128,1024]{1,0:T(8,128)(2,1)S(1)}, bf16[128,1024]{1,0:T(8,128)(2,1)}, bf16[128,1024]{1,0:T(8,128)(2,1)S(1)}, bf16[128,1024]{1,0:T(8,128)(2,1)}) fusion(bf16[1,128,4096]{2,1,0:T(8,128)(2,1)} %param.7, s32[]{:T(128)S(6)} %select_n.109, s32[]{:T(128)S(6)} %select_n.105, s32[]{:T(128)S(6)} %select_n.98, s32[]{:T(128)S(6)} %select_n.107), kind=kLoop, calls=%fused_computation.6 | loop fusion | bytes 2097168 | tf_op jit(solution)/shard_map/dynamic_slice | solution.py:229
  104.7 1.5 collective-permute-start
  106.2 1.4 collective-permute-start.30
  108.3 1.0 copy-done.2
  109.3 0.9 copy-done.4
  110.2 1.1 copy-done.7
  111.3 1.1 copy-done.9
  112.4 0.9 copy-done.11
  116.1 0.9 copy-done.23
  119.7 4.4 %project.2.refs_5_.refs_6_ = bf16[384,512]{1,0:T(8,128)(2,1)S(1)} custom-call(s32[3]{0:T(128)S(1)} %pad_add_fusion.refs_0_, bf16[128,5120]{1,0:T(8,128)(2,1)S(1)} %bitcast.50, bf16[64,5120]{1,0:T(8,128)(2,1)S(1)} %copy-done.7, bf16[64,5120]{1,0:T(8,128)(2,1)} %collective-permute-done.2.refs_3_, bf16[64,5120]{1,0:T(8,128)(2,1)} %collective-permute-done.3.refs_4_, ...), custom_call_target="tpu_custom_call" | custom-call | flops 2013265920 | bytes 18874368 | tf_op jit(solution)/shard_map/project/pallas_call | solution.py:63
  124.3 3.2 %project.3.refs_6_.refs_7_ = bf16[128,512]{1,0:T(8,128)(2,1)S(1)} custom-call(s32[3]{0:T(128)S(1)} %pad_add_fusion.refs_0_, bf16[64,5120]{1,0:T(8,128)(2,1)} %collective-permute-done.22.refs_1_, bf16[64,5120]{1,0:T(8,128)(2,1)} %collective-permute-done.23.refs_2_, bf16[3,160,512]{2,1,0:T(8,128)(2,1)S(1)} %pad_maximum_fusion.refs_6_.refs_3_, ...), custom_call_target="tpu_custom_call" | custom-call | flops 671088640 | bytes 18874368 | tf_op jit(solution)/shard_map/project/pallas_call | solution.py:63
  127.5 2.1 %collective-permute-start.27 = (bf16[128,512]{1,0:T(8,128)(2,1)S(1)}, bf16[128,512]{1,0:T(8,128)(2,1)S(1)}, u32[]{:S(2)}, u32[]{:S(2)}) collective-permute-start(bf16[128,512]{1,0:T(8,128)(2,1)S(1)} %project.3.refs_6_.refs_7_), channel_id=1, source_target_pairs={{0,2},{2,0},{1,3},{3,1},{4,6},{6,4},{5,7},{7,5},{8,10},{10,8},{9,1... | collective-permute-start | bytes 393224 | tf_op jit(solution)/shard_map/ppermute | solution.py:30
  130.4 6.7 %collective-permute-done.27.refs_10_.refs_11_ = bf16[128,512]{1,0:T(8,128)(2,1)S(1)} collective-permute-done((bf16[128,512]{1,0:T(8,128)(2,1)S(1)}, bf16[128,512]{1,0:T(8,128)(2,1)S(1)}, u32[]{:S(2)}, u32[]{:S(2)}) %collective-permute-start.27) | collective-permute-done | bytes 131104 | tf_op jit(solution)/shard_map/ppermute | solution.py:30
  138.8 1.1 collective-permute-done.29.refs_12_.refs_13_
  140.1 0.9 copy-done.32
  141.0 4.0 %attend.3 = (bf16[128,1024]{1,0:T(8,128)(2,1)S(1)}, f32[2,2,16,256]{3,2,1,0:T(8,128)S(1)}) custom-call(s32[24]{0:T(128)S(1)} %concatenate.6.refs_0_, s32[4,128,128]{2,1,0:T(8,128)S(1)} %broadcast_in_dim.45.refs_1_, bf16[4,16,128]{2,1,0:T(8,128)(2,1)S(1)} %select_convert_fusion.refs_2_, f32[2,2,16,256]{3,2,1,0:T(8,128)S(1)} %broadcast_in_dim.48.refs_3_, ...), custom_call_target="tpu_custom_call" | custom-call | flops 367001600 | bytes 12582912 | tf_op jit(solution)/shard_map/attend/pallas_call | solution.py:160
  145.0 5.1 %attend.4 = (bf16[128,1024]{1,0:T(8,128)(2,1)S(1)}, bf16[128,1024]{1,0:T(8,128)(2,1)S(1)}, f32[2,2,16,256]{3,2,1,0:T(8,128)S(1)}) custom-call(s32[24]{0:T(128)S(1)} %concatenate.6.refs_0_, s32[4,128,128]{2,1,0:T(8,128)S(1)} %broadcast_in_dim.45.refs_1_, bf16[4,16,128]{2,1,0:T(8,128)(2,1)S(1)} %select_convert_fusion.refs_2_, ...), custom_call_target="tpu_custom_call" | custom-call | flops 734003200 | bytes 25165824 | tf_op jit(solution)/shard_map/attend/pallas_call | solution.py:160
  150.1 2.1 %attend.5 = (bf16[128,1024]{1,0:T(8,128)(2,1)S(1)}, f32[2,2,16,256]{3,2,1,0:T(8,128)S(1)}) custom-call(s32[24]{0:T(128)S(1)} %concatenate.6.refs_0_, s32[4,128,128]{2,1,0:T(8,128)S(1)} %broadcast_in_dim.45.refs_1_, bf16[4,16,128]{2,1,0:T(8,128)(2,1)S(1)} %select_convert_fusion.refs_2_, f32[2,2,16,256]{3,2,1,0:T(8,128)S(1)} %get-tuple-element.10.refs_3_, ...), custom_call_target="tpu_custom_call" | custom-call | flops 367001600 | bytes 12582912 | tf_op jit(solution)/shard_map/attend/pallas_call | solution.py:160
  153.1 2.6 %collective-permute-start.32 = (bf16[128,1024]{1,0:T(8,128)(2,1)S(1)}, bf16[128,1024]{1,0:T(8,128)(2,1)S(1)}, u32[]{:S(2)}, u32[]{:S(2)}) collective-permute-start(bf16[128,1024]{1,0:T(8,128)(2,1)S(1)} %get-tuple-element.12), channel_id=1, source_target_pairs={{0,12},{4,0},{8,4},{12,8},{1,13},{5,1},{9,5},{13,9},{2,14},{6,2},{... | collective-permute-start | bytes 786440 | tf_op jit(solution)/shard_map/ppermute | solution.py:30
  155.7 1.5 collective-permute-start.34
  157.3 3.7 %collective-permute-done.36 = f32[16,256]{1,0:T(8,128)S(1)} collective-permute-done((f32[16,256]{1,0:T(8,128)S(1)}, f32[16,256]{1,0:T(8,128)S(1)}, u32[]{:S(2)}, u32[]{:S(2)}) %collective-permute-start.36) | collective-permute-done | bytes 16416 | tf_op jit(solution)/shard_map/ppermute | solution.py:30
  161.7 5.5 %collective-permute-done.32.refs_1_ = bf16[128,1024]{1,0:T(8,128)(2,1)S(1)} collective-permute-done((bf16[128,1024]{1,0:T(8,128)(2,1)S(1)}, bf16[128,1024]{1,0:T(8,128)(2,1)S(1)}, u32[]{:S(2)}, u32[]{:S(2)}) %collective-permute-start.32) | collective-permute-done | bytes 262176 | tf_op jit(solution)/shard_map/ppermute | solution.py:30
  167.2 3.4 %collective-permute-done.33.refs_2_ = bf16[128,1024]{1,0:T(8,128)(2,1)S(1)} collective-permute-done((bf16[128,1024]{1,0:T(8,128)(2,1)S(1)}, bf16[128,1024]{1,0:T(8,128)(2,1)S(1)}, u32[]{:S(2)}, u32[]{:S(2)}) %collective-permute-start.33) | collective-permute-done | bytes 262176 | tf_op jit(solution)/shard_map/ppermute | solution.py:30
  170.5 1.6 assemble.1
  (135 shorter events, 21.0 us)
Async XLA Ops:
  0.6 30.5 %copy-start = (bf16[1,128,5120]{2,1,0:T(8,128)(2,1)S(1)}, bf16[1,128,5120]{2,1,0:T(8,128)(2,1)}, u32[]{:S(2)}) copy-start(bf16[1,128,5120]{2,1,0:T(8,128)(2,1)} %param.6) | copy-start | bytes 3932164
  1.7 15.2 %collective-permute-start.10 = (bf16[160,512]{1,0:T(8,128)(2,1)S(1)}, bf16[160,512]{1,0:T(8,128)(2,1)S(1)}, u32[]{:S(2)}, u32[]{:S(2)}) collective-permute-start(bf16[160,512]{1,0:T(8,128)(2,1)S(1)} %get-tuple-element.28), channel_id=1, source_target_pairs={{0,32},{16,48},{32,0},{48,16},{1,33},{17,49},{33,1},{49,17},{2,34}... | collective-permute-start | bytes 491528 | tf_op jit(solution)/shard_map/ppermute | solution.py:30
  9.0 11.6 %collective-permute-start.5 = (bf16[160,512]{1,0:T(8,128)(2,1)S(1)}, bf16[160,512]{1,0:T(8,128)(2,1)S(1)}, u32[]{:S(2)}, u32[]{:S(2)}) collective-permute-start(bf16[160,512]{1,0:T(8,128)(2,1)S(1)} %get-tuple-element.28), channel_id=1, source_target_pairs={{0,16},{16,32},{32,48},{48,0},{1,17},{17,33},{33,49},{49,1},{2,18}... | collective-permute-start | bytes 491528 | tf_op jit(solution)/shard_map/ppermute | solution.py:30
  10.5 13.9 %collective-permute-start.6 = (bf16[160,512]{1,0:T(8,128)(2,1)S(1)}, bf16[160,512]{1,0:T(8,128)(2,1)S(1)}, u32[]{:S(2)}, u32[]{:S(2)}) collective-permute-start(bf16[160,512]{1,0:T(8,128)(2,1)S(1)} %get-tuple-element.28), channel_id=1, source_target_pairs={{0,48},{16,0},{32,16},{48,32},{1,49},{17,1},{33,17},{49,33},{2,50}... | collective-permute-start | bytes 491528 | tf_op jit(solution)/shard_map/ppermute | solution.py:30
  16.9 38.9 %copy-start.10 = (bf16[160,512]{1,0:T(8,128)(2,1)}, bf16[160,512]{1,0:T(8,128)(2,1)S(1)}, u32[]{:S(2)}) copy-start(bf16[160,512]{1,0:T(8,128)(2,1)S(1)} %collective-permute-done.10.refs_10_.refs_7_) | copy-start | bytes 491524
  16.9 12.7 %collective-permute-start.11 = (bf16[160,512]{1,0:T(8,128)(2,1)S(1)}, bf16[160,512]{1,0:T(8,128)(2,1)S(1)}, u32[]{:S(2)}, u32[]{:S(2)}) collective-permute-start(bf16[160,512]{1,0:T(8,128)(2,1)S(1)} %collective-permute-done.10.refs_10_.refs_7_), channel_id=1, source_target_pairs={{0,64},{64,128},{128,192},{192,0},{1,65},{65,129},{129,193},{193,1... | collective-permute-start | bytes 491528 | tf_op jit(solution)/shard_map/ppermute | solution.py:30
  24.4 7.9 %copy-start.33 = (s32[1,16]{1,0:T(1,128)S(1)}, s32[1,16]{1,0:T(1,128)}, u32[]{:S(2)}) copy-start(s32[1,16]{1,0:T(1,128)} %param.9) | copy-start | bytes 196
  24.4 32.9 %copy-start.34 = (s32[1,16]{1,0:T(1,128)S(1)}, s32[1,16]{1,0:T(1,128)}, u32[]{:S(2)}) copy-start(s32[1,16]{1,0:T(1,128)} %param.10) | copy-start | bytes 196
  24.4 36.1 %copy-start.35 = (s32[4]{0:T(128)S(1)}, s32[4]{0:T(128)}, u32[]{:S(2)}) copy-start(s32[4]{0:T(128)} %constant.145.clone) | copy-start | bytes 52
  24.4 40.6 %collective-permute-start.7 = (bf16[3,160,512]{2,1,0:T(8,128)(2,1)S(1)}, bf16[3,160,512]{2,1,0:T(8,128)(2,1)S(1)}, u32[]{:S(2)}, u32[]{:S(2)}) collective-permute-start(bf16[3,160,512]{2,1,0:T(8,128)(2,1)S(1)} %pad_maximum_fusion.refs_6_.refs_3_), channel_id=1, source_target_pairs={{0,64},{64,128},{128,192},{192,0},{1,65},{65,129},{129,193},{193,1... | collective-permute-start | bytes 1474568 | tf_op jit(solution)/shard_map/ppermute | solution.py:30
  26.1 40.5 %collective-permute-start.8 = (bf16[3,160,512]{2,1,0:T(8,128)(2,1)S(1)}, bf16[3,160,512]{2,1,0:T(8,128)(2,1)S(1)}, u32[]{:S(2)}, u32[]{:S(2)}) collective-permute-start(bf16[3,160,512]{2,1,0:T(8,128)(2,1)S(1)} %pad_maximum_fusion.refs_6_.refs_3_), channel_id=1, source_target_pairs={{0,128},{64,192},{128,0},{192,64},{1,129},{65,193},{129,1},{193,65... | collective-permute-start | bytes 1474568 | tf_op jit(solution)/shard_map/ppermute | solution.py:30
  27.0 40.1 %collective-permute-start.9 = (bf16[3,160,512]{2,1,0:T(8,128)(2,1)S(1)}, bf16[3,160,512]{2,1,0:T(8,128)(2,1)}, u32[]{:S(2)}, u32[]{:S(2)}) collective-permute-start(bf16[3,160,512]{2,1,0:T(8,128)(2,1)S(1)} %pad_maximum_fusion.refs_6_.refs_3_), channel_id=1, source_target_pairs={{0,192},{64,0},{128,64},{192,128},{1,193},{65,1},{129,65},{193,129... | collective-permute-start | bytes 1474568 | tf_op jit(solution)/shard_map/ppermute | solution.py:30
  29.4 26.3 %collective-permute-start.12 = (bf16[160,512]{1,0:T(8,128)(2,1)S(1)}, bf16[160,512]{1,0:T(8,128)(2,1)S(1)}, u32[]{:S(2)}, u32[]{:S(2)}) collective-permute-start(bf16[160,512]{1,0:T(8,128)(2,1)S(1)} %collective-permute-done.10.refs_10_.refs_7_), channel_id=1, source_target_pairs={{0,128},{64,192},{128,0},{192,64},{1,129},{65,193},{129,1},{193,65... | collective-permute-start | bytes 491528 | tf_op jit(solution)/shard_map/ppermute | solution.py:30
  29.6 27.6 %copy-start.13 = (bf16[160,512]{1,0:T(8,128)(2,1)}, bf16[160,512]{1,0:T(8,128)(2,1)S(1)}, u32[]{:S(2)}) copy-start(bf16[160,512]{1,0:T(8,128)(2,1)S(1)} %collective-permute-done.11.refs_11_.refs_8_) | copy-start | bytes 491524
  29.6 27.6 %collective-permute-start.13 = (bf16[160,512]{1,0:T(8,128)(2,1)S(1)}, bf16[160,512]{1,0:T(8,128)(2,1)S(1)}, u32[]{:S(2)}, u32[]{:S(2)}) collective-permute-start(bf16[160,512]{1,0:T(8,128)(2,1)S(1)} %collective-permute-done.10.refs_10_.refs_7_), channel_id=1, source_target_pairs={{0,192},{64,0},{128,64},{192,128},{1,193},{65,1},{129,65},{193,129... | collective-permute-start | bytes 491528 | tf_op jit(solution)/shard_map/ppermute | solution.py:30
  55.8 1.5 collective-permute-start.18
  57.3 1.9 %collective-permute-start.19 = (bf16[160,512]{1,0:T(8,128)(2,1)S(1)}, bf16[160,512]{1,0:T(8,128)(2,1)S(1)}, u32[]{:S(2)}, u32[]{:S(2)}) collective-permute-start(bf16[160,512]{1,0:T(8,128)(2,1)S(1)} %collective-permute-done.11.refs_11_.refs_8_), channel_id=1, source_target_pairs={{0,1},{1,0},{2,3},{3,2},{4,5},{5,4},{6,7},{7,6},{8,9},{9,8},{10,11... | collective-permute-start | bytes 491528 | tf_op jit(solution)/shard_map/ppermute | solution.py:30
  58.0 2.5 %collective-permute-start.20 = (bf16[160,512]{1,0:T(8,128)(2,1)S(1)}, bf16[160,512]{1,0:T(8,128)(2,1)S(1)}, u32[]{:S(2)}, u32[]{:S(2)}) collective-permute-start(bf16[160,512]{1,0:T(8,128)(2,1)S(1)} %collective-permute-done.12.refs_12_.refs_9_), channel_id=1, source_target_pairs={{0,1},{1,0},{2,3},{3,2},{4,5},{5,4},{6,7},{7,6},{8,9},{9,8},{10,11... | collective-permute-start | bytes 491528 | tf_op jit(solution)/shard_map/ppermute | solution.py:30
  59.8 2.9 %collective-permute-start.21 = (bf16[160,512]{1,0:T(8,128)(2,1)S(1)}, bf16[160,512]{1,0:T(8,128)(2,1)S(1)}, u32[]{:S(2)}, u32[]{:S(2)}) collective-permute-start(bf16[160,512]{1,0:T(8,128)(2,1)S(1)} %collective-permute-done.13.refs_13_.refs_10_), channel_id=1, source_target_pairs={{0,1},{1,0},{2,3},{3,2},{4,5},{5,4},{6,7},{7,6},{8,9},{9,8},{10,11... | collective-permute-start | bytes 491528 | tf_op jit(solution)/shard_map/ppermute | solution.py:30
  61.2 19.1 %collective-permute-start.3 = (bf16[64,5120]{1,0:T(8,128)(2,1)}, bf16[64,5120]{1,0:T(8,128)(2,1)}, u32[]{:S(2)}, u32[]{:S(2)}) collective-permute-start(bf16[64,5120]{1,0:T(8,128)(2,1)} %get-tuple-element.22), channel_id=1, source_target_pairs={{0,4},{4,8},{8,12},{12,0},{1,5},{5,9},{9,13},{13,1},{2,6},{6,10},{... | collective-permute-start | bytes 1966088 | tf_op jit(solution)/shard_map/ppermute | solution.py:30
  63.3 31.2 %collective-permute-start.1 = (bf16[64,5120]{1,0:T(8,128)(2,1)}, bf16[64,5120]{1,0:T(8,128)(2,1)S(1)}, u32[]{:S(2)}, u32[]{:S(2)}) collective-permute-start(bf16[64,5120]{1,0:T(8,128)(2,1)} %get-tuple-element.22), channel_id=1, source_target_pairs={{0,12},{4,0},{8,4},{12,8},{1,13},{5,1},{9,5},{13,9},{2,14},{6,2},{... | collective-permute-start | bytes 1966088 | tf_op jit(solution)/shard_map/ppermute | solution.py:30
  65.1 29.5 %collective-permute-start.2 = (bf16[64,5120]{1,0:T(8,128)(2,1)}, bf16[64,5120]{1,0:T(8,128)(2,1)}, u32[]{:S(2)}, u32[]{:S(2)}) collective-permute-start(bf16[64,5120]{1,0:T(8,128)(2,1)} %get-tuple-element.21), channel_id=1, source_target_pairs={{0,12},{4,0},{8,4},{12,8},{1,13},{5,1},{9,5},{13,9},{2,14},{6,2},{... | collective-permute-start | bytes 1966088 | tf_op jit(solution)/shard_map/ppermute | solution.py:30
  66.6 30.3 %collective-permute-start.4 = (bf16[64,5120]{1,0:T(8,128)(2,1)}, bf16[64,5120]{1,0:T(8,128)(2,1)S(1)}, u32[]{:S(2)}, u32[]{:S(2)}) collective-permute-start(bf16[64,5120]{1,0:T(8,128)(2,1)} %get-tuple-element.21), channel_id=1, source_target_pairs={{0,4},{4,8},{8,12},{12,0},{1,5},{5,9},{9,13},{13,1},{2,6},{6,10},{... | collective-permute-start | bytes 1966088 | tf_op jit(solution)/shard_map/ppermute | solution.py:30
  67.1 1.9 %collective-permute-start.14 = (bf16[3,160,512]{2,1,0:T(8,128)(2,1)S(1)}, bf16[3,160,512]{2,1,0:T(8,128)(2,1)S(1)}, u32[]{:S(2)}, u32[]{:S(2)}) collective-permute-start(bf16[3,160,512]{2,1,0:T(8,128)(2,1)S(1)} %pad_maximum_fusion.refs_6_.refs_3_), channel_id=1, source_target_pairs={{0,1},{1,0},{2,3},{3,2},{4,5},{5,4},{6,7},{7,6},{8,9},{9,8},{10,11... | collective-permute-start | bytes 1474568 | tf_op jit(solution)/shard_map/ppermute | solution.py:30
  69.8 34.9 %collective-permute-start.15 = (bf16[3,160,512]{2,1,0:T(8,128)(2,1)S(1)}, bf16[3,160,512]{2,1,0:T(8,128)(2,1)}, u32[]{:S(2)}, u32[]{:S(2)}) collective-permute-start(bf16[3,160,512]{2,1,0:T(8,128)(2,1)S(1)} %collective-permute-done.7.refs_7_.refs_4_), channel_id=1, source_target_pairs={{0,1},{1,0},{2,3},{3,2},{4,5},{5,4},{6,7},{7,6},{8,9},{9,8},{10,11... | collective-permute-start | bytes 1474568 | tf_op jit(solution)/shard_map/ppermute | solution.py:30
  80.3 25.9 %collective-permute-start.16 = (bf16[3,160,512]{2,1,0:T(8,128)(2,1)S(1)}, bf16[3,160,512]{2,1,0:T(8,128)(2,1)}, u32[]{:S(2)}, u32[]{:S(2)}) collective-permute-start(bf16[3,160,512]{2,1,0:T(8,128)(2,1)S(1)} %collective-permute-done.8.refs_8_.refs_5_), channel_id=1, source_target_pairs={{0,1},{1,0},{2,3},{3,2},{4,5},{5,4},{6,7},{7,6},{8,9},{9,8},{10,11... | collective-permute-start | bytes 1474568 | tf_op jit(solution)/shard_map/ppermute | solution.py:30
  94.5 13.1 %collective-permute-start.17 = (bf16[3,160,512]{2,1,0:T(8,128)(2,1)}, bf16[3,160,512]{2,1,0:T(8,128)(2,1)}, u32[]{:S(2)}, u32[]{:S(2)}) collective-permute-start(bf16[3,160,512]{2,1,0:T(8,128)(2,1)} %collective-permute-done.9.refs_9_.refs_6_), channel_id=1, source_target_pairs={{0,1},{1,0},{2,3},{3,2},{4,5},{5,4},{6,7},{7,6},{8,9},{9,8},{10,11... | collective-permute-start | bytes 1474568 | tf_op jit(solution)/shard_map/ppermute | solution.py:30
  95.4 28.8 %collective-permute-start.22 = (bf16[64,5120]{1,0:T(8,128)(2,1)}, bf16[64,5120]{1,0:T(8,128)(2,1)}, u32[]{:S(2)}, u32[]{:S(2)}) collective-permute-start(bf16[64,5120]{1,0:T(8,128)(2,1)} %collective-permute-done.3.refs_4_), channel_id=1, source_target_pairs={{0,4},{4,8},{8,12},{12,0},{1,5},{5,9},{9,13},{13,1},{2,6},{6,10},{... | collective-permute-start | bytes 1966088 | tf_op jit(solution)/shard_map/ppermute | solution.py:30
  97.7 26.5 %collective-permute-start.23 = (bf16[64,5120]{1,0:T(8,128)(2,1)}, bf16[64,5120]{1,0:T(8,128)(2,1)}, u32[]{:S(2)}, u32[]{:S(2)}) collective-permute-start(bf16[64,5120]{1,0:T(8,128)(2,1)} %collective-permute-done.2.refs_3_), channel_id=1, source_target_pairs={{0,12},{4,0},{8,4},{12,8},{1,13},{5,1},{9,5},{13,9},{2,14},{6,2},{... | collective-permute-start | bytes 1966088 | tf_op jit(solution)/shard_map/ppermute | solution.py:30
  102.5 5.7 %copy-start.5 = (f32[384,128]{1,0:T(8,128)S(1)}, f32[384,128]{1,0:T(8,128)}, u32[]{:S(2)}) copy-start(f32[384,128]{1,0:T(8,128)} %slice.37.refs_23_) | copy-start | bytes 589828
  104.7 25.0 %collective-permute-start = (bf16[128,1024]{1,0:T(8,128)(2,1)S(1)}, bf16[128,1024]{1,0:T(8,128)(2,1)S(1)}, u32[]{:S(2)}, u32[]{:S(2)}) collective-permute-start(bf16[128,1024]{1,0:T(8,128)(2,1)S(1)} %get-tuple-element.25), channel_id=1, source_target_pairs={{0,8},{4,12},{8,0},{12,4},{1,9},{5,13},{9,1},{13,5},{2,10},{6,14},... | collective-permute-start | bytes 786440 | tf_op jit(solution)/shard_map/ppermute | solution.py:30
  106.2 38.8 %collective-permute-start.30 = (bf16[128,1024]{1,0:T(8,128)(2,1)}, bf16[128,1024]{1,0:T(8,128)(2,1)}, u32[]{:S(2)}, u32[]{:S(2)}) collective-permute-start(bf16[128,1024]{1,0:T(8,128)(2,1)} %get-tuple-element.24), channel_id=1, source_target_pairs={{0,12},{4,0},{8,4},{12,8},{1,13},{5,1},{9,5},{13,9},{2,14},{6,2},{... | collective-permute-start | bytes 786440 | tf_op jit(solution)/shard_map/ppermute | solution.py:30
  107.7 37.4 %collective-permute-start.31 = (bf16[128,1024]{1,0:T(8,128)(2,1)}, bf16[128,1024]{1,0:T(8,128)(2,1)}, u32[]{:S(2)}, u32[]{:S(2)}) collective-permute-start(bf16[128,1024]{1,0:T(8,128)(2,1)} %get-tuple-element.26), channel_id=1, source_target_pairs={{0,4},{4,8},{8,12},{12,0},{1,5},{5,9},{9,13},{13,1},{2,6},{6,10},{... | collective-permute-start | bytes 786440 | tf_op jit(solution)/shard_map/ppermute | solution.py:30
  119.7 4.6 %copy-start.15 = (bf16[160,512]{1,0:T(8,128)(2,1)S(1)}, bf16[160,512]{1,0:T(8,128)(2,1)}, u32[]{:S(2)}) copy-start(bf16[160,512]{1,0:T(8,128)(2,1)} %copy-done.13) | copy-start | bytes 491524
  119.7 4.6 %copy-start.18 = (bf16[160,512]{1,0:T(8,128)(2,1)S(1)}, bf16[160,512]{1,0:T(8,128)(2,1)}, u32[]{:S(2)}) copy-start(bf16[160,512]{1,0:T(8,128)(2,1)} %copy-done.16) | copy-start | bytes 491524
  119.7 4.6 %copy-start.21 = (bf16[160,512]{1,0:T(8,128)(2,1)S(1)}, bf16[160,512]{1,0:T(8,128)(2,1)}, u32[]{:S(2)}) copy-start(bf16[160,512]{1,0:T(8,128)(2,1)} %copy-done.19) | copy-start | bytes 491524
  119.7 4.6 %copy-start.30 = (f32[128,128]{1,0:T(8,128)S(1)}, f32[128,128]{1,0:T(8,128)}, u32[]{:S(2)}) copy-start(f32[128,128]{1,0:T(8,128)} %slice.39.refs_20_) | copy-start | bytes 196612
  124.2 13.0 %collective-permute-start.26 = (bf16[384,512]{1,0:T(8,128)(2,1)S(1)}, bf16[384,512]{1,0:T(8,128)(2,1)S(1)}, u32[]{:S(2)}, u32[]{:S(2)}) collective-permute-start(bf16[384,512]{1,0:T(8,128)(2,1)S(1)} %project.2.refs_5_.refs_6_), channel_id=1, source_target_pairs={{0,2},{2,0},{1,3},{3,1},{4,6},{6,4},{5,7},{7,5},{8,10},{10,8},{9,1... | collective-permute-start | bytes 1179656 | tf_op jit(solution)/shard_map/ppermute | solution.py:30
  127.5 9.7 %collective-permute-start.27 = (bf16[128,512]{1,0:T(8,128)(2,1)S(1)}, bf16[128,512]{1,0:T(8,128)(2,1)S(1)}, u32[]{:S(2)}, u32[]{:S(2)}) collective-permute-start(bf16[128,512]{1,0:T(8,128)(2,1)S(1)} %project.3.refs_6_.refs_7_), channel_id=1, source_target_pairs={{0,2},{2,0},{1,3},{3,1},{4,6},{6,4},{5,7},{7,5},{8,10},{10,8},{9,1... | collective-permute-start | bytes 393224 | tf_op jit(solution)/shard_map/ppermute | solution.py:30
  130.4 8.3 %collective-permute-start.24 = (bf16[384,512]{1,0:T(8,128)(2,1)S(1)}, bf16[384,512]{1,0:T(8,128)(2,1)S(1)}, u32[]{:S(2)}, u32[]{:S(2)}) collective-permute-start(bf16[384,512]{1,0:T(8,128)(2,1)S(1)} %project.2.refs_5_.refs_6_), channel_id=1, source_target_pairs={{0,1},{1,0},{2,3},{3,2},{4,5},{5,4},{6,7},{7,6},{8,9},{9,8},{10,11... | collective-permute-start | bytes 1179656 | tf_op jit(solution)/shard_map/ppermute | solution.py:30
  137.2 1.3 collective-permute-start.25
  137.2 2.7 %collective-permute-start.28 = (bf16[384,512]{1,0:T(8,128)(2,1)S(1)}, bf16[384,512]{1,0:T(8,128)(2,1)S(1)}, u32[]{:S(2)}, u32[]{:S(2)}) collective-permute-start(bf16[384,512]{1,0:T(8,128)(2,1)S(1)} %collective-permute-done.26.refs_9_.refs_10_), channel_id=1, source_target_pairs={{0,1},{1,0},{2,3},{3,2},{4,5},{5,4},{6,7},{7,6},{8,9},{9,8},{10,11... | collective-permute-start | bytes 1179656 | tf_op jit(solution)/shard_map/ppermute | solution.py:30
  138.5 1.3 collective-permute-start.29
  152.2 5.0 %collective-permute-start.35 = (f32[2,16,256]{2,1,0:T(8,128)S(1)}, f32[2,16,256]{2,1,0:T(8,128)S(1)}, u32[]{:S(2)}, u32[]{:S(2)}) collective-permute-start(f32[2,16,256]{2,1,0:T(8,128)S(1)} %dynamic-slice_bitcast_fusion.4), channel_id=1, source_target_pairs={{0,1},{1,0},{2,3},{3,2},{4,5},{5,4},{6,7},{7,6},{8,9},{9,8},{10,11... | collective-permute-start | bytes 98312 | tf_op jit(solution)/shard_map/ppermute | solution.py:30
  153.1 14.1 %collective-permute-start.32 = (bf16[128,1024]{1,0:T(8,128)(2,1)S(1)}, bf16[128,1024]{1,0:T(8,128)(2,1)S(1)}, u32[]{:S(2)}, u32[]{:S(2)}) collective-permute-start(bf16[128,1024]{1,0:T(8,128)(2,1)S(1)} %get-tuple-element.12), channel_id=1, source_target_pairs={{0,12},{4,0},{8,4},{12,8},{1,13},{5,1},{9,5},{13,9},{2,14},{6,2},{... | collective-permute-start | bytes 786440 | tf_op jit(solution)/shard_map/ppermute | solution.py:30
  155.7 14.8 %collective-permute-start.33 = (bf16[128,1024]{1,0:T(8,128)(2,1)S(1)}, bf16[128,1024]{1,0:T(8,128)(2,1)S(1)}, u32[]{:S(2)}, u32[]{:S(2)}) collective-permute-start(bf16[128,1024]{1,0:T(8,128)(2,1)S(1)} %get-tuple-element.13), channel_id=1, source_target_pairs={{0,4},{4,8},{8,12},{12,0},{1,5},{5,9},{9,13},{13,1},{2,6},{6,10},{... | collective-permute-start | bytes 786440 | tf_op jit(solution)/shard_map/ppermute | solution.py:30
  155.7 14.8 %collective-permute-start.34 = (bf16[128,1024]{1,0:T(8,128)(2,1)S(1)}, bf16[128,1024]{1,0:T(8,128)(2,1)S(1)}, u32[]{:S(2)}, u32[]{:S(2)}) collective-permute-start(bf16[128,1024]{1,0:T(8,128)(2,1)S(1)} %get-tuple-element.14), channel_id=1, source_target_pairs={{0,8},{4,12},{8,0},{12,4},{1,9},{5,13},{9,1},{13,5},{2,10},{6,14},... | collective-permute-start | bytes 786440 | tf_op jit(solution)/shard_map/ppermute | solution.py:30
  157.2 3.8 %collective-permute-start.36 = (f32[16,256]{1,0:T(8,128)S(1)}, f32[16,256]{1,0:T(8,128)S(1)}, u32[]{:S(2)}, u32[]{:S(2)}) collective-permute-start(f32[16,256]{1,0:T(8,128)S(1)} %dynamic-slice_bitcast_fusion.5), channel_id=1, source_target_pairs={{0,2},{2,0},{1,3},{3,1},{4,6},{6,4},{5,7},{7,5},{8,10},{10,8},{9,1... | collective-permute-start | bytes 49160 | tf_op jit(solution)/shard_map/ppermute | solution.py:30
  (25 other events, 28.7 us)
where the time goes:
time: 174 us; the launch traced here: 172 us
  waiting for transfers between devices  81.8 us (47%)
  starting transfers between devices  40.3 us (23%)
  local copies, waits for them, and re-layouts  26.4 us (15%)
  Pallas kernels  20.3 us (12%)
  other arithmetic  2.34 us (1%)
    ppermute x37, waiting for transfers between devices, shift(): return lax.ppermute(v, axis, [(i, (i + d) % n) for i in range(n)])  81.8 us
    ppermute x37, starting transfers between devices, shift(): return lax.ppermute(v, axis, [(i, (i + d) % n) for i in range(n)])  40.3 us
    unnamed x72, local copies, waits for them, and re-layouts  19.6 us
    pallas_call x3, Pallas kernels, attend(): pl.pallas_call(functools.partial(attn_kernel, js), out_shape=[jax.ShapeDt...  11.2 us
    pallas_call x2, Pallas kernels, project(): pl.pallas_call(functools.partial(proj_kernel, len(pieces)), out_shape=jax...  7.59 us
  transfers between devices with their start and end apart: 37, of which 14 were waited for; matrix products, arithmetic and copies ran while one was open for 5% of the time, Pallas kernels for 7%

commit v1 on v0

--- a/solution.py
+++ b/solution.py
@@ -2,6 +2,7 @@
 
 import jax
 import jax.numpy as jnp
+import numpy as np
 from jax import lax
 from jax.experimental import pallas as pl
 from jax.experimental.pallas import tpu as pltpu
@@ -25,16 +26,68 @@
 CHUNK = 256
 
 
+VM = pl.BlockSpec(memory_space=pltpu.VMEM)
+SM = pl.BlockSpec(memory_space=pltpu.SMEM)
+
+
 def shift(v, axis, d):
     n = lax.axis_size(axis)
     return lax.ppermute(v, axis, [(i, (i + d) % n) for i in range(n)])
 
 
-def proj_kernel(n, *refs):
+TURNS = (0, 1, 3, 2)
+
+
+def block_of(idx, k):
+    turn = (idx[0] + TURNS[k]) & 3
+    return turn * 4 + idx[1] * 2 + idx[2]
+
+
+def starts_of(lengths):
+    starts = [jnp.int32(0)]
+    for r in range(DOCS):
+        starts.append(starts[r] + lengths[0, r])
+    return starts
+
+
+def begin_of(token, starts):
+    begin = jnp.zeros_like(token)
+    for r in range(1, DOCS):
+        begin = jnp.where(token >= starts[r], starts[r], begin)
+    return begin
+
+
+def table_kernel(idx, lengths, freq_ref, cos_ref, sin_ref):
+    starts = starts_of(lengths)
+    row = lax.broadcasted_iota(jnp.int32, (TOK, HEAD), 0)
+    lane = lax.broadcasted_iota(jnp.int32, (TOK, HEAD), 1)
+    for k in range(4):
+        token = row + block_of(idx, k) * TOK
+        angle = (token - begin_of(token, starts)).astype(F32) * freq_ref[...]
+        rows = slice(k * TOK, (k + 1) * TOK)
+        cos_ref[rows, :] = jnp.cos(angle)
+        sine = jnp.sin(angle)
+        sin_ref[rows, :] = jnp.where(lane < HEAD // 2, -sine, sine)
+
+
+def tables(idx, lengths, freq):
+    out = jax.ShapeDtypeStruct((4 * TOK, HEAD), F32)
+    return pl.pallas_call(
+        table_kernel,
+        out_shape=[out, out],
+        in_specs=[SM, SM, VM],
+        out_specs=[VM, VM],
+        compiler_params=pltpu.CompilerParams(vmem_limit_bytes=4 * MIB),
+        cost_estimate=pl.CostEstimate(flops=1 << 22, bytes_accessed=MIB, transcendentals=1 << 17),
+        name="tables",
+    )(idx, lengths, freq)
+
+
+def proj_kernel(n, first, *refs):
     idx, hs, refs = refs[0], refs[1 : 1 + n], refs[1 + n :]
     sets, refs = (refs[:8], refs[8:16]), refs[16:]
     cos_ref, sin_ref, out_ref, wbuf, acc = refs
-    core, zh, my_y = idx[0], idx[1], idx[2]
+    core, zh, my_y = idx[2], idx[3], idx[4]
     span = 4 * ROWS
     for d in range(4):
         for m, c in enumerate((core, 1 - core)):
@@ -49,7 +102,8 @@
         elif d < 3:
             acc[...] = acc[...] + p
     p = acc[...] + p
-    cos, sin = cos_ref[...], sin_ref[...]
+    rows = slice(first, first + p.shape[0])
+    cos, sin = cos_ref[rows, :], sin_ref[rows, :]
     for k in range(4):
         v = p[:, k * HEAD : (k + 1) * HEAD]
         if k < 2:
@@ -57,11 +111,11 @@
         out_ref[:, k * HEAD : (k + 1) * HEAD] = v.astype(BF)
 
 
-def project(idx, pieces, weights, cos, sin):
+def project(idx, first, pieces, weights, cos, sin):
     row = sum(h.shape[0] for h in pieces)
     vm = pl.BlockSpec(memory_space=pltpu.VMEM)
     return pl.pallas_call(
-        functools.partial(proj_kernel, len(pieces)),
+        functools.partial(proj_kernel, len(pieces), first),
         out_shape=jax.ShapeDtypeStruct((row, COLS), BF),
         in_specs=[pl.BlockSpec(memory_space=pltpu.SMEM)] + [vm] * (len(pieces) + 18),
         out_specs=vm,
@@ -79,13 +133,14 @@
 
 def attn_kernel(js, *refs):
     n = len(js)
-    idx, qs_ref, mem_ref, prev_ref = refs[:4]
+    idx, lengths, wanted, prev_ref = refs[:4]
     q_refs, kv_in, refs = refs[4 : 4 + n], refs[4 + n : 12 + n], refs[12 + n :]
+    starts = starts_of(lengths)
     o_refs, refs = refs[:n], refs[n:]
     pool_ref, kvbuf, sbuf, mx, ls, acc = refs
     for g in range(4):
         for j in range(4):
-            to = pl.ds(pl.multiple_of(idx[g * 4 + j] * TOK, TOK), TOK)
+            to = pl.ds(pl.multiple_of((block_of(idx, j) ^ g) * TOK, TOK), TOK)
             row = j % 3 * TOK
             kvbuf[to, :] = kv_in[2 * g + j // 3][row : row + TOK, :]
     kvbuf[pl.ds(16 * TOK, TOK), :] = jnp.zeros((TOK, COLS), BF)
@@ -94,9 +149,11 @@
     factor = HEAD ** (-0.5) * LOG2E
     total = jnp.zeros((DOCS, OCOLS), F32)
     for t, j in enumerate(js):
-        lo, hi = idx[16 + j], idx[20 + j]
-        n_chunks = (hi - lo) // 2 + 1
-        first = jnp.concatenate([qs_ref[j], qs_ref[j]], axis=1) - lane
+        hi = block_of(idx, j)
+        lo = lax.shift_right_logical(begin_of(hi * TOK, starts), 7)
+        n_chunks = lax.shift_right_logical(hi - lo, 1) + 1
+        begin = begin_of(row[:, :TOK] + hi * TOK, starts)
+        first = jnp.concatenate([begin, begin], axis=1) - lane
         last = row - lane + hi * TOK
         mx[...] = jnp.full((2, 4 * TOK, TOK), NEG, F32)
         ls[...] = jnp.zeros((2, 4 * TOK, TOK), F32)
@@ -148,20 +205,27 @@
             for g in range(4):
                 h = (e * 4 + g) * HEAD
                 o_refs[t][:, h : h + HEAD] = o[g * TOK : (g + 1) * TOK]
-        total = total + jnp.dot(mem_ref[j], o_refs[t][...], preferred_element_type=F32)
+        doc = lax.broadcasted_iota(jnp.int32, (DOCS, TOK), 0)
+        token = lax.broadcasted_iota(jnp.int32, (DOCS, TOK), 1) + hi * TOK
+        member = jnp.zeros((DOCS, TOK), F32)
+        for r in range(DOCS):
+            answer = jnp.minimum(wanted[0, r], lengths[0, r])
+            inside = (token >= starts[r + 1] - answer) & (token < starts[r + 1])
+            member = jnp.where((doc == r) & inside, 1.0, member)
+        total = total + jnp.dot(member.astype(BF), o_refs[t][...], preferred_element_type=F32)
     for zc in range(4):
         part = total[:, zc * 256 : zc * 256 + 256]
         pool_ref[zc % 2, zc // 2] = prev_ref[zc % 2, zc // 2] + part
 
 
-def attend(js, idx, qs, starts, member, prev, kv):
+def attend(js, idx, lengths, wanted, prev, qs, kv):
     n = len(js)
     vm = pl.BlockSpec(memory_space=pltpu.VMEM)
     out = pl.pallas_call(
         functools.partial(attn_kernel, js),
         out_shape=[jax.ShapeDtypeStruct((TOK, OCOLS), BF)] * n
         + [jax.ShapeDtypeStruct((2, 2, DOCS, 256), F32)],
-        in_specs=[pl.BlockSpec(memory_space=pltpu.SMEM)] + [vm] * (11 + n),
+        in_specs=[SM] * 3 + [vm] * (9 + n),
         out_specs=[vm] * (n + 1),
         scratch_shapes=[
             pltpu.VMEM((17 * TOK, COLS), BF),
@@ -175,14 +239,14 @@
             flops=n * 2 * 2 * 1024 * 700 * 128, bytes_accessed=n * 12 * MIB, transcendentals=n * 700 * 1024
         ),
         name="attend",
-    )(idx, starts, member, prev, *[qs[j] for j in js], *kv)
+    )(idx, lengths, wanted, prev, *[qs[j] for j in js], *kv)
     return out[:n], out[n]
 
 
 def assemble_kernel(idx, *refs):
     ins, out_ref = refs[:4], refs[4]
     for d in range(4):
-        lo = pl.multiple_of(idx[d] * OCOLS, OCOLS)
+        lo = pl.multiple_of(((idx[0] + d) & 3) * OCOLS, OCOLS)
         out_ref[0, :, pl.ds(lo, OCOLS)] = ins[d][...]
 
 
@@ -201,11 +265,16 @@
 
 def program(hidden, queries, weight, doc_lengths, resp_lengths):
     x, zl, core = lax.axis_index("x"), lax.axis_index("zl"), lax.axis_index("c")
-    zh, rest = lax.axis_index("zh"), 2 * zl + core
-    h, q = hidden[0], queries[0]
-
-    keys = lax.dynamic_slice(weight, (core * HALF, x * 256), (HALF, 256))
-    vals = lax.dynamic_slice(weight, (core * HALF, OCOLS + x * 256), (HALF, 256))
+    info = jnp.stack([x, zl, core, lax.axis_index("zh"), lax.axis_index("y")]).astype(jnp.int32)
+    spots = [((x + d) & 3) * OCOLS for d in range(4)]
+    scalars = (x * 256, OCOLS + x * 256, core * HALF, core, 1 - core, zl, 1 - zl, *spots)
+    scalars = [v.astype(jnp.uint32) for v in scalars]
+    weight, q, info, *scalars = lax.optimization_barrier((weight, queries[0], info, *scalars))
+    key_at, value_at, row_at, core, other_core, zl, other_zl, *spots = scalars
+    h = hidden[0]
+
+    keys = lax.dynamic_slice(weight, (row_at, key_at), (HALF, 256))
+    vals = lax.dynamic_slice(weight, (row_at, value_at), (HALF, 256))
     own = jnp.concatenate([keys, vals], axis=1)
     z1 = shift(own, "zh", 1)
     z3 = shift(own, "zh", -1)
@@ -226,41 +295,19 @@
         mine[4 + d] = shift(z2, "y", d)
     weights = mine + [shift(v, "c", 1) for v in mine]
 
-    give = lambda d: lax.dynamic_slice(q, (0, (x + d) % 4 * OCOLS), (TOK, OCOLS))
-    gives = [give(d) for d in range(4)]
+    gives = [lax.dynamic_slice(q, (jnp.uint32(0), at), (TOK, OCOLS)) for at in spots]
     q1 = shift(gives[3], "x", -1)
     q3 = shift(gives[1], "x", 1)
     q2 = shift(gives[2], "x", 2)
     qs = [gives[0], q1, q3, q2]
 
-    lengths, wanted = doc_lengths[0], resp_lengths[0]
-    ends = jnp.cumsum(lengths)
-    starts = ends - lengths
-    answer = jnp.minimum(wanted, lengths)
-    turn = (x + jnp.array([0, 1, 3, 2], jnp.int32)) % 4
-    block = turn * 4 + rest
-    token = (block[:, None] * TOK + jnp.arange(TOK, dtype=jnp.int32)[None, :])[:, :, None]
-    inside = (token >= starts) & (token < ends)
-    begin = jnp.sum(jnp.where(inside, starts, 0), axis=2)
-    member = jnp.where(inside & (token >= ends - answer), 1.0, 0.0).astype(BF)
-    member = jnp.swapaxes(member, 1, 2)
-    position = token[:, :, 0] - begin
-    pair = jnp.arange(HEAD, dtype=jnp.int32) % (HEAD // 2)
-    freq = ROPE_BASE ** (-(pair.astype(F32) * 2.0 / HEAD))
-    angle = position.reshape(4 * TOK).astype(F32)[:, None] * freq
-    cosine = jnp.cos(angle)
-    sine = jnp.where(jnp.arange(HEAD) < HEAD // 2, -1.0, 1.0) * jnp.sin(angle)
-    spread = jnp.broadcast_to(begin[:, :, None], (4, TOK, TOK))
-    places = jnp.concatenate([(block ^ m) for m in range(4)])
-    aidx = jnp.concatenate([places, begin[:, 0] // TOK, block]).astype(jnp.int32)
-    widx = jnp.stack([core, zh, lax.axis_index("y")]).astype(jnp.int32)
-
-    cos0, cos1 = cosine[: 3 * TOK], cosine[3 * TOK :]
-    sin0, sin1 = sine[: 3 * TOK], sine[3 * TOK :]
+    freq = ROPE_BASE ** (-(np.arange(HEAD) % (HEAD // 2)) * 2.0 / HEAD)
+    cosine, sine = tables(info, doc_lengths, jnp.asarray(freq.astype(np.float32)[None]))
+
     near = [h, top_right, bottom_right, top_left, bottom_left]
-    kv_near = project(widx, near, weights, cos0, sin0)
+    kv_near = project(info, 0, near, weights, cosine, sine)
     kv_near_z = shift(kv_near, "zl", 1)
-    kv_far = project(widx, [far_top, far_bottom], weights, cos1, sin1)
+    kv_far = project(info, 3 * TOK, [far_top, far_bottom], weights, cosine, sine)
     kv_far_z = shift(kv_far, "zl", 1)
     kv = []
     for near, far in ((kv_near, kv_far), (kv_near_z, kv_far_z)):
@@ -268,17 +315,19 @@
     kv = kv[0] + kv[1]
 
     pool = jnp.zeros((2, 2, DOCS, 256), F32)
-    (o3,), pool = attend((3,), aidx, qs, spread, member, pool, kv)
+    (o3,), pool = attend((3,), info, doc_lengths, resp_lengths, pool, qs, kv)
     r3 = shift(o3, "x", 2)
-    (o1, o2), pool = attend((1, 2), aidx, qs, spread, member, pool, kv)
+    (o1, o2), pool = attend((1, 2), info, doc_lengths, resp_lengths, pool, qs, kv)
     r2 = shift(o1, "x", 1)
     r1 = shift(o2, "x", -1)
-    (o0,), pool = attend((0,), aidx, qs, spread, member, pool, kv)
-    attended = assemble(turn.astype(jnp.int32), [o0, r1, r2, r3])
-
-    pick = lambda v, i: lax.dynamic_index_in_dim(v, i, 0, keepdims=False)
-    sums = pick(pool, core) + shift(pick(pool, 1 - core), "c", 1)
-    sums = pick(sums, zl) + shift(pick(sums, 1 - zl), "zl", 1)
+    (o0,), pool = attend((0,), info, doc_lengths, resp_lengths, pool, qs, kv)
+    attended = assemble(info, [o0, r1, r3, r2])
+
+    zero = jnp.uint32(0)
+    pick = lambda v, i: lax.dynamic_slice(v, (i,) + (zero,) * (v.ndim - 1), (1, *v.shape[1:]))[0]
+    sums = pick(pool, core) + shift(pick(pool, other_core), "c", 1)
+    sums = pick(sums, zl) + shift(pick(sums, other_zl), "zl", 1)
+    answer = jnp.minimum(resp_lengths[0], doc_lengths[0])
     pooled = sums / answer.astype(F32)[:, None]
     return attended, pooled[None]
 

time: 174 us -> 134 us (0.77)
  the two profiles are of different devices: /device:TPU:8 before, /device:TPU:1 now
where the time goes in v1:
time: 134 us
  starting transfers between devices  62.7 us (47%)
  waiting for transfers between devices  50.7 us (38%)
  Pallas kernels  16.8 us (13%)
  local copies, waits for them, and re-layouts  2.16 us (2%)
    ppermute x37, starting transfers between devices, shift(): return lax.ppermute(v, axis, [(i, (i + d) % n) for i in range(n)])  62.7 us
    ppermute x37, waiting for transfers between devices, shift(): return lax.ppermute(v, axis, [(i, (i + d) % n) for i in range(n)])  50.7 us
    pallas_call x3, Pallas kernels, attend(): pl.pallas_call(functools.partial(attn_kernel, js), out_shape=[jax.ShapeDt...  8.66 us
    pallas_call x2, Pallas kernels, project(): pl.pallas_call(functools.partial(proj_kernel, len(pieces), first), out_sh...  4.8 us
  transfers between devices with their start and end apart: 37, of which 13 were waited for; matrix products, arithmetic and copies ran while one was open for 1% of the time, Pallas kernels for 6%

profile of v1, /device:TPU:1, one launch (start us, length us, event | category | flops | bytes accessed | tf_op | source)
XLA Modules:
  0.0 134.0 jit_solution(1926403225853966768)
XLA Ops:
  0.7 1.2 fusion.3
  2.0 7.8 %collective-permute-start.10 = (bf16[160,512]{1,0:T(8,128)(2,1)S(1)}, bf16[160,512]{1,0:T(8,128)(2,1)S(1)}, u32[]{:S(2)}, u32[]{:S(2)}) collective-permute-start(bf16[160,512]{1,0:T(8,128)(2,1)S(1)} %get-tuple-element.57), channel_id=1, source_target_pairs={{0,32},{16,48},{32,0},{48,16},{1,33},{17,49},{33,1},{49,17},{2,34}... | collective-permute-start | bytes 491528 | tf_op jit(solution)/shard_map/ppermute | solution.py:35
  9.8 1.2 collective-permute-start.5
  11.0 2.3 %collective-permute-done.10.refs_10_.refs_7_ = bf16[160,512]{1,0:T(8,128)(2,1)S(1)} collective-permute-done((bf16[160,512]{1,0:T(8,128)(2,1)S(1)}, bf16[160,512]{1,0:T(8,128)(2,1)S(1)}, u32[]{:S(2)}, u32[]{:S(2)}) %collective-permute-start.10) | collective-permute-done | bytes 163872 | tf_op jit(solution)/shard_map/ppermute | solution.py:35
  13.2 1.7 %collective-permute-start.11 = (bf16[160,512]{1,0:T(8,128)(2,1)S(1)}, bf16[160,512]{1,0:T(8,128)(2,1)S(1)}, u32[]{:S(2)}, u32[]{:S(2)}) collective-permute-start(bf16[160,512]{1,0:T(8,128)(2,1)S(1)} %collective-permute-done.10.refs_10_.refs_7_), channel_id=1, source_target_pairs={{0,64},{64,128},{128,192},{192,0},{1,65},{65,129},{129,193},{193,1... | collective-permute-start | bytes 491528 | tf_op jit(solution)/shard_map/ppermute | solution.py:35
  15.0 7.6 %collective-permute-start.6 = (bf16[160,512]{1,0:T(8,128)(2,1)S(1)}, bf16[160,512]{1,0:T(8,128)(2,1)S(1)}, u32[]{:S(2)}, u32[]{:S(2)}) collective-permute-start(bf16[160,512]{1,0:T(8,128)(2,1)S(1)} %get-tuple-element.57), channel_id=1, source_target_pairs={{0,48},{16,0},{32,16},{48,32},{1,49},{17,1},{33,17},{49,33},{2,50}... | collective-permute-start | bytes 491528 | tf_op jit(solution)/shard_map/ppermute | solution.py:35
  22.6 2.6 %collective-permute-start.12 = (bf16[160,512]{1,0:T(8,128)(2,1)S(1)}, bf16[160,512]{1,0:T(8,128)(2,1)S(1)}, u32[]{:S(2)}, u32[]{:S(2)}) collective-permute-start(bf16[160,512]{1,0:T(8,128)(2,1)S(1)} %collective-permute-done.10.refs_10_.refs_7_), channel_id=1, source_target_pairs={{0,128},{64,192},{128,0},{192,64},{1,129},{65,193},{129,1},{193,65... | collective-permute-start | bytes 491528 | tf_op jit(solution)/shard_map/ppermute | solution.py:35
  25.2 1.1 collective-permute-start.13
  26.3 4.0 %collective-permute-start.18 = (bf16[160,512]{1,0:T(8,128)(2,1)S(1)}, bf16[160,512]{1,0:T(8,128)(2,1)S(1)}, u32[]{:S(2)}, u32[]{:S(2)}) collective-permute-start(bf16[160,512]{1,0:T(8,128)(2,1)S(1)} %collective-permute-done.10.refs_10_.refs_7_), channel_id=1, source_target_pairs={{0,1},{1,0},{2,3},{3,2},{4,5},{5,4},{6,7},{7,6},{8,9},{9,8},{10,11... | collective-permute-start | bytes 491528 | tf_op jit(solution)/shard_map/ppermute | solution.py:35
  30.5 0.5 collective-permute-start.7
  31.0 0.5 collective-permute-start.8
  31.5 2.0 %collective-permute-start.9 = (bf16[3,160,512]{2,1,0:T(8,128)(2,1)S(1)}, bf16[3,160,512]{2,1,0:T(8,128)(2,1)S(1)}, u32[]{:S(2)}, u32[]{:S(2)}) collective-permute-start(bf16[3,160,512]{2,1,0:T(8,128)(2,1)S(1)} %pad_maximum_fusion.refs_6_.refs_3_), channel_id=1, source_target_pairs={{0,192},{64,0},{128,64},{192,128},{1,193},{65,1},{129,65},{193,129... | collective-permute-start | bytes 1474568 | tf_op jit(solution)/shard_map/ppermute | solution.py:35
  33.5 3.8 %collective-permute-start.20 = (bf16[160,512]{1,0:T(8,128)(2,1)S(1)}, bf16[160,512]{1,0:T(8,128)(2,1)S(1)}, u32[]{:S(2)}, u32[]{:S(2)}) collective-permute-start(bf16[160,512]{1,0:T(8,128)(2,1)S(1)} %collective-permute-done.12.refs_12_.refs_9_), channel_id=1, source_target_pairs={{0,1},{1,0},{2,3},{3,2},{4,5},{5,4},{6,7},{7,6},{8,9},{9,8},{10,11... | collective-permute-start | bytes 491528 | tf_op jit(solution)/shard_map/ppermute | solution.py:35
  37.4 0.8 collective-permute-done.20.refs_20_.refs_17_
  38.3 1.2 collective-permute-start.3
  39.5 1.6 %collective-permute-start.2 = (bf16[64,5120]{1,0:T(8,128)(2,1)S(1)}, bf16[64,5120]{1,0:T(8,128)(2,1)S(1)}, u32[]{:S(2)}, u32[]{:S(2)}) collective-permute-start(bf16[64,5120]{1,0:T(8,128)(2,1)S(1)} %get-tuple-element.50), channel_id=1, source_target_pairs={{0,12},{4,0},{8,4},{12,8},{1,13},{5,1},{9,5},{13,9},{2,14},{6,2},{... | collective-permute-start | bytes 1966088 | tf_op jit(solution)/shard_map/ppermute | solution.py:35
  41.1 13.5 %collective-permute-done.7.refs_7_.refs_4_ = bf16[3,160,512]{2,1,0:T(8,128)(2,1)S(1)} collective-permute-done((bf16[3,160,512]{2,1,0:T(8,128)(2,1)S(1)}, bf16[3,160,512]{2,1,0:T(8,128)(2,1)S(1)}, u32[]{:S(2)}, u32[]{:S(2)}) %collective-permute-start.7) | collective-permute-done | bytes 491552 | tf_op jit(solution)/shard_map/ppermute | solution.py:35
  54.6 1.3 collective-permute-start.14
  56.0 2.5 %collective-permute-start.1 = (bf16[64,5120]{1,0:T(8,128)(2,1)S(1)}, bf16[64,5120]{1,0:T(8,128)(2,1)S(1)}, u32[]{:S(2)}, u32[]{:S(2)}) collective-permute-start(bf16[64,5120]{1,0:T(8,128)(2,1)S(1)} %get-tuple-element.51), channel_id=1, source_target_pairs={{0,12},{4,0},{8,4},{12,8},{1,13},{5,1},{9,5},{13,9},{2,14},{6,2},{... | collective-permute-start | bytes 1966088 | tf_op jit(solution)/shard_map/ppermute | solution.py:35
  59.3 13.2 %collective-permute-done.1.refs_2_ = bf16[64,5120]{1,0:T(8,128)(2,1)S(1)} collective-permute-done((bf16[64,5120]{1,0:T(8,128)(2,1)S(1)}, bf16[64,5120]{1,0:T(8,128)(2,1)S(1)}, u32[]{:S(2)}, u32[]{:S(2)}) %collective-permute-start.1) | collective-permute-done | bytes 655392 | tf_op jit(solution)/shard_map/ppermute | solution.py:35
  72.5 0.9 collective-permute-start.22
  73.5 2.2 %collective-permute-done.4.refs_5_ = bf16[64,5120]{1,0:T(8,128)(2,1)S(1)} collective-permute-done((bf16[64,5120]{1,0:T(8,128)(2,1)S(1)}, bf16[64,5120]{1,0:T(8,128)(2,1)S(1)}, u32[]{:S(2)}, u32[]{:S(2)}) %collective-permute-start.4) | collective-permute-done | bytes 655392 | tf_op jit(solution)/shard_map/ppermute | solution.py:35
  75.9 1.8 %tables.1 = (f32[512,128]{1,0:T(8,128)S(1)}, f32[512,128]{1,0:T(8,128)S(1)}) custom-call(s32[5]{0:T(128)S(1)} %stack.35.idx.refs_0_, s32[1,16]{1,0:T(1,128)S(1)} %copy-done.1, f32[1,128]{1,0:T(1,128)S(1)} %copy-done.3), custom_call_target="tpu_custom_call" | custom-call | flops 4194304 | bytes 1048576 | tf_op jit(solution)/shard_map/tables/pallas_call | solution.py:75
  77.8 3.0 %project.2.refs_5_.refs_6_ = bf16[384,512]{1,0:T(8,128)(2,1)S(1)} custom-call(s32[5]{0:T(128)S(1)} %stack.35.idx.refs_0_, bf16[128,5120]{1,0:T(8,128)(2,1)S(1)} %bitcast.31, bf16[64,5120]{1,0:T(8,128)(2,1)S(1)} %collective-permute-done.1.refs_2_, bf16[64,5120]{1,0:T(8,128)(2,1)S(1)} %collective-permute-done.2.refs_3_, ...), custom_call_target="tpu_custom_call" | custom-call | flops 2013265920 | bytes 18874368 | tf_op jit(solution)/shard_map/project/pallas_call | solution.py:117
  80.9 0.8 constant_dynamic-slice_fusion
  81.6 1.3 collective-permute-start
  82.9 1.4 %collective-permute-start.24 = (bf16[384,512]{1,0:T(8,128)(2,1)S(1)}, bf16[384,512]{1,0:T(8,128)(2,1)S(1)}, u32[]{:S(2)}, u32[]{:S(2)}) collective-permute-start(bf16[384,512]{1,0:T(8,128)(2,1)S(1)} %project.2.refs_5_.refs_6_), channel_id=1, source_target_pairs={{0,1},{1,0},{2,3},{3,2},{4,5},{5,4},{6,7},{7,6},{8,9},{9,8},{10,11... | collective-permute-start | bytes 1179656 | tf_op jit(solution)/shard_map/ppermute | solution.py:35
  84.4 6.0 %collective-permute-done.26.refs_9_.refs_10_ = bf16[384,512]{1,0:T(8,128)(2,1)S(1)} collective-permute-done((bf16[384,512]{1,0:T(8,128)(2,1)S(1)}, bf16[384,512]{1,0:T(8,128)(2,1)S(1)}, u32[]{:S(2)}, u32[]{:S(2)}) %collective-permute-start.26) | collective-permute-done | bytes 393248 | tf_op jit(solution)/shard_map/ppermute | solution.py:35
  90.4 2.0 %collective-permute-start.28 = (bf16[384,512]{1,0:T(8,128)(2,1)S(1)}, bf16[384,512]{1,0:T(8,128)(2,1)S(1)}, u32[]{:S(2)}, u32[]{:S(2)}) collective-permute-start(bf16[384,512]{1,0:T(8,128)(2,1)S(1)} %collective-permute-done.26.refs_9_.refs_10_), channel_id=1, source_target_pairs={{0,1},{1,0},{2,3},{3,2},{4,5},{5,4},{6,7},{7,6},{8,9},{9,8},{10,11... | collective-permute-start | bytes 1179656 | tf_op jit(solution)/shard_map/ppermute | solution.py:35
  92.4 1.8 %project.3.refs_6_.refs_7_ = bf16[128,512]{1,0:T(8,128)(2,1)S(1)} custom-call(s32[5]{0:T(128)S(1)} %stack.35.idx.refs_0_, bf16[64,5120]{1,0:T(8,128)(2,1)S(1)} %collective-permute-done.22.refs_1_, bf16[64,5120]{1,0:T(8,128)(2,1)S(1)} %collective-permute-done.23.refs_2_, bf16[3,160,512]{2,1,0:T(8,128)(2,1)S(1)} %pad_maximum_fusion.refs_6_.refs_3_, ...), custom_call_target="tpu_custom_call" | custom-call | flops 671088640 | bytes 18874368 | tf_op jit(solution)/shard_map/project/pallas_call | solution.py:117
  94.3 2.1 %collective-permute-start.25 = (bf16[128,512]{1,0:T(8,128)(2,1)S(1)}, bf16[128,512]{1,0:T(8,128)(2,1)S(1)}, u32[]{:S(2)}, u32[]{:S(2)}) collective-permute-start(bf16[128,512]{1,0:T(8,128)(2,1)S(1)} %project.3.refs_6_.refs_7_), channel_id=1, source_target_pairs={{0,1},{1,0},{2,3},{3,2},{4,5},{5,4},{6,7},{7,6},{8,9},{9,8},{10,11... | collective-permute-start | bytes 393224 | tf_op jit(solution)/shard_map/ppermute | solution.py:35
  96.7 2.1 %collective-permute-start.30 = (bf16[128,1024]{1,0:T(8,128)(2,1)S(1)}, bf16[128,1024]{1,0:T(8,128)(2,1)S(1)}, u32[]{:S(2)}, u32[]{:S(2)}) collective-permute-start(bf16[128,1024]{1,0:T(8,128)(2,1)S(1)} %get-tuple-element.54), channel_id=1, source_target_pairs={{0,12},{4,0},{8,4},{12,8},{1,13},{5,1},{9,5},{13,9},{2,14},{6,2},{... | collective-permute-start | bytes 786440 | tf_op jit(solution)/shard_map/ppermute | solution.py:35
  98.8 1.6 %collective-permute-start.31 = (bf16[128,1024]{1,0:T(8,128)(2,1)S(1)}, bf16[128,1024]{1,0:T(8,128)(2,1)S(1)}, u32[]{:S(2)}, u32[]{:S(2)}) collective-permute-start(bf16[128,1024]{1,0:T(8,128)(2,1)S(1)} %get-tuple-element.53), channel_id=1, source_target_pairs={{0,4},{4,8},{8,12},{12,0},{1,5},{5,9},{9,13},{13,1},{2,6},{6,10},{... | collective-permute-start | bytes 786440 | tf_op jit(solution)/shard_map/ppermute | solution.py:35
  100.5 1.2 collective-permute-start.29
  101.7 1.0 collective-permute-done.29.refs_12_.refs_13_
  102.7 2.1 %attend.3 = (bf16[128,1024]{1,0:T(8,128)(2,1)S(1)}, f32[2,2,16,256]{3,2,1,0:T(8,128)S(1)}) custom-call(s32[5]{0:T(128)S(1)} %stack.35.idx.refs_0_, s32[1,16]{1,0:T(1,128)S(1)} %copy-done.1, s32[1,16]{1,0:T(1,128)S(1)} %copy-done.2, f32[2,2,16,256]{3,2,1,0:T(8,128)S(1)} %broadcast_in_dim.7.refs_3_, bf16[128,1024]{1,0:T(8,128)(2,1)S(1)} %collective-permute-done.refs_4_, ...), custom_call_target="tpu_custom_call" | custom-call | flops 367001600 | bytes 12582912 | tf_op jit(solution)/shard_map/attend/pallas_call | solution.py:224
  105.2 4.5 %attend.4 = (bf16[128,1024]{1,0:T(8,128)(2,1)S(1)}, bf16[128,1024]{1,0:T(8,128)(2,1)S(1)}, f32[2,2,16,256]{3,2,1,0:T(8,128)S(1)}) custom-call(s32[5]{0:T(128)S(1)} %stack.35.idx.refs_0_, s32[1,16]{1,0:T(1,128)S(1)} %copy-done.1, s32[1,16]{1,0:T(1,128)S(1)} %copy-done.2, f32[2,2,16,256]{3,2,1,0:T(8,128)S(1)} %get-tuple-element.34.refs_3_, ...), custom_call_target="tpu_custom_call" | custom-call | flops 734003200 | bytes 25165824 | tf_op jit(solution)/shard_map/attend/pallas_call | solution.py:224
  109.8 2.1 %attend.5 = (bf16[128,1024]{1,0:T(8,128)(2,1)S(1)}, f32[2,2,16,256]{3,2,1,0:T(8,128)S(1)}) custom-call(s32[5]{0:T(128)S(1)} %stack.35.idx.refs_0_, s32[1,16]{1,0:T(1,128)S(1)} %copy-done.1, s32[1,16]{1,0:T(1,128)S(1)} %copy-done.2, f32[2,2,16,256]{3,2,1,0:T(8,128)S(1)} %get-tuple-element.37.refs_3_, bf16[128,1024]{1,0:T(8,128)(2,1)S(1)} %get-tuple-element.52.refs_4_, ...), custom_call_target="tpu_custom_call" | custom-call | flops 367001600 | bytes 12582912 | tf_op jit(solution)/shard_map/attend/pallas_call | solution.py:224
  111.8 4.3 %collective-permute-start.35 = (f32[2,16,256]{2,1,0:T(8,128)S(1)}, f32[2,16,256]{2,1,0:T(8,128)S(1)}, u32[]{:S(2)}, u32[]{:S(2)}) collective-permute-start(f32[2,16,256]{2,1,0:T(8,128)S(1)} %dynamic-slice_bitcast_fusion), channel_id=1, source_target_pairs={{0,1},{1,0},{2,3},{3,2},{4,5},{5,4},{6,7},{7,6},{8,9},{9,8},{10,11... | collective-permute-start | bytes 98312 | tf_op jit(solution)/shard_map/ppermute | solution.py:35
  116.2 1.3 %collective-permute-start.32 = (bf16[128,1024]{1,0:T(8,128)(2,1)S(1)}, bf16[128,1024]{1,0:T(8,128)(2,1)S(1)}, u32[]{:S(2)}, u32[]{:S(2)}) collective-permute-start(bf16[128,1024]{1,0:T(8,128)(2,1)S(1)} %get-tuple-element.40), channel_id=1, source_target_pairs={{0,12},{4,0},{8,4},{12,8},{1,13},{5,1},{9,5},{13,9},{2,14},{6,2},{... | collective-permute-start | bytes 786440 | tf_op jit(solution)/shard_map/ppermute | solution.py:35
  117.5 0.9 collective-permute-start.34
  118.4 2.4 %collective-permute-start.33 = (bf16[128,1024]{1,0:T(8,128)(2,1)S(1)}, bf16[128,1024]{1,0:T(8,128)(2,1)S(1)}, u32[]{:S(2)}, u32[]{:S(2)}) collective-permute-start(bf16[128,1024]{1,0:T(8,128)(2,1)S(1)} %get-tuple-element.41), channel_id=1, source_target_pairs={{0,8},{4,12},{8,0},{12,4},{1,9},{5,13},{9,1},{13,5},{2,10},{6,14},... | collective-permute-start | bytes 786440 | tf_op jit(solution)/shard_map/ppermute | solution.py:35
  120.9 2.9 %collective-permute-done.36 = f32[16,256]{1,0:T(8,128)S(1)} collective-permute-done((f32[16,256]{1,0:T(8,128)S(1)}, f32[16,256]{1,0:T(8,128)S(1)}, u32[]{:S(2)}, u32[]{:S(2)}) %collective-permute-start.36) | collective-permute-done | bytes 16416 | tf_op jit(solution)/shard_map/ppermute | solution.py:35
  123.7 0.7 fusion.1
  124.4 0.5 collective-permute-done.32.refs_1_
  125.0 1.2 collective-permute-done.34.refs_3_
  126.2 6.2 %collective-permute-done.33.refs_2_ = bf16[128,1024]{1,0:T(8,128)(2,1)S(1)} collective-permute-done((bf16[128,1024]{1,0:T(8,128)(2,1)S(1)}, bf16[128,1024]{1,0:T(8,128)(2,1)S(1)}, u32[]{:S(2)}, u32[]{:S(2)}) %collective-permute-start.33) | collective-permute-done | bytes 262176 | tf_op jit(solution)/shard_map/ppermute | solution.py:35
  132.4 1.6 %assemble.1 = bf16[1,128,4096]{2,1,0:T(8,128)(2,1)} custom-call(s32[5]{0:T(128)S(1)} %stack.35.idx.refs_0_, bf16[128,1024]{1,0:T(8,128)(2,1)S(1)} %get-tuple-element.39.refs_0_, bf16[128,1024]{1,0:T(8,128)(2,1)S(1)} %collective-permute-done.32.refs_1_, bf16[128,1024]{1,0:T(8,128)(2,1)S(1)} %collective-permute-done.33.refs_2_, ...), custom_call_target="tpu_custom_call" | custom-call | bytes 2097152 | tf_op jit(solution)/shard_map/assemble/pallas_call | solution.py:255
  (55 shorter events, 2.8 us)
Async XLA Ops:
  0.6 36.7 %copy-start = (bf16[1,128,5120]{2,1,0:T(8,128)(2,1)S(1)}, bf16[1,128,5120]{2,1,0:T(8,128)(2,1)}, u32[]{:S(2)}) copy-start(bf16[1,128,5120]{2,1,0:T(8,128)(2,1)} %param.6) | copy-start | bytes 3932164
  2.0 11.3 %collective-permute-start.10 = (bf16[160,512]{1,0:T(8,128)(2,1)S(1)}, bf16[160,512]{1,0:T(8,128)(2,1)S(1)}, u32[]{:S(2)}, u32[]{:S(2)}) collective-permute-start(bf16[160,512]{1,0:T(8,128)(2,1)S(1)} %get-tuple-element.57), channel_id=1, source_target_pairs={{0,32},{16,48},{32,0},{48,16},{1,33},{17,49},{33,1},{49,17},{2,34}... | collective-permute-start | bytes 491528 | tf_op jit(solution)/shard_map/ppermute | solution.py:35
  9.8 16.5 %collective-permute-start.5 = (bf16[160,512]{1,0:T(8,128)(2,1)S(1)}, bf16[160,512]{1,0:T(8,128)(2,1)S(1)}, u32[]{:S(2)}, u32[]{:S(2)}) collective-permute-start(bf16[160,512]{1,0:T(8,128)(2,1)S(1)} %get-tuple-element.57), channel_id=1, source_target_pairs={{0,16},{16,32},{32,48},{48,0},{1,17},{17,33},{33,49},{49,1},{2,18}... | collective-permute-start | bytes 491528 | tf_op jit(solution)/shard_map/ppermute | solution.py:35
  13.2 17.1 %collective-permute-start.11 = (bf16[160,512]{1,0:T(8,128)(2,1)S(1)}, bf16[160,512]{1,0:T(8,128)(2,1)S(1)}, u32[]{:S(2)}, u32[]{:S(2)}) collective-permute-start(bf16[160,512]{1,0:T(8,128)(2,1)S(1)} %collective-permute-done.10.refs_10_.refs_7_), channel_id=1, source_target_pairs={{0,64},{64,128},{128,192},{192,0},{1,65},{65,129},{129,193},{193,1... | collective-permute-start | bytes 491528 | tf_op jit(solution)/shard_map/ppermute | solution.py:35
  15.0 15.4 %collective-permute-start.6 = (bf16[160,512]{1,0:T(8,128)(2,1)S(1)}, bf16[160,512]{1,0:T(8,128)(2,1)S(1)}, u32[]{:S(2)}, u32[]{:S(2)}) collective-permute-start(bf16[160,512]{1,0:T(8,128)(2,1)S(1)} %get-tuple-element.57), channel_id=1, source_target_pairs={{0,48},{16,0},{32,16},{48,32},{1,49},{17,1},{33,17},{49,33},{2,50}... | collective-permute-start | bytes 491528 | tf_op jit(solution)/shard_map/ppermute | solution.py:35
  22.6 8.4 %collective-permute-start.12 = (bf16[160,512]{1,0:T(8,128)(2,1)S(1)}, bf16[160,512]{1,0:T(8,128)(2,1)S(1)}, u32[]{:S(2)}, u32[]{:S(2)}) collective-permute-start(bf16[160,512]{1,0:T(8,128)(2,1)S(1)} %collective-permute-done.10.refs_10_.refs_7_), channel_id=1, source_target_pairs={{0,128},{64,192},{128,0},{192,64},{1,129},{65,193},{129,1},{193,65... | collective-permute-start | bytes 491528 | tf_op jit(solution)/shard_map/ppermute | solution.py:35
  25.2 6.3 %collective-permute-start.13 = (bf16[160,512]{1,0:T(8,128)(2,1)S(1)}, bf16[160,512]{1,0:T(8,128)(2,1)S(1)}, u32[]{:S(2)}, u32[]{:S(2)}) collective-permute-start(bf16[160,512]{1,0:T(8,128)(2,1)S(1)} %collective-permute-done.10.refs_10_.refs_7_), channel_id=1, source_target_pairs={{0,192},{64,0},{128,64},{192,128},{1,193},{65,1},{129,65},{193,129... | collective-permute-start | bytes 491528 | tf_op jit(solution)/shard_map/ppermute | solution.py:35
  26.3 7.2 %collective-permute-start.18 = (bf16[160,512]{1,0:T(8,128)(2,1)S(1)}, bf16[160,512]{1,0:T(8,128)(2,1)S(1)}, u32[]{:S(2)}, u32[]{:S(2)}) collective-permute-start(bf16[160,512]{1,0:T(8,128)(2,1)S(1)} %collective-permute-done.10.refs_10_.refs_7_), channel_id=1, source_target_pairs={{0,1},{1,0},{2,3},{3,2},{4,5},{5,4},{6,7},{7,6},{8,9},{9,8},{10,11... | collective-permute-start | bytes 491528 | tf_op jit(solution)/shard_map/ppermute | solution.py:35
  30.3 6.9 %collective-permute-start.19 = (bf16[160,512]{1,0:T(8,128)(2,1)S(1)}, bf16[160,512]{1,0:T(8,128)(2,1)S(1)}, u32[]{:S(2)}, u32[]{:S(2)}) collective-permute-start(bf16[160,512]{1,0:T(8,128)(2,1)S(1)} %collective-permute-done.11.refs_11_.refs_8_), channel_id=1, source_target_pairs={{0,1},{1,0},{2,3},{3,2},{4,5},{5,4},{6,7},{7,6},{8,9},{9,8},{10,11... | collective-permute-start | bytes 491528 | tf_op jit(solution)/shard_map/ppermute | solution.py:35
  30.5 45.5 %copy-start.1 = (s32[1,16]{1,0:T(1,128)S(1)}, s32[1,16]{1,0:T(1,128)}, u32[]{:S(2)}) copy-start(s32[1,16]{1,0:T(1,128)} %refs_1_.5) | copy-start | bytes 196
  30.5 45.5 %copy-start.3 = (f32[1,128]{1,0:T(1,128)S(1)}, f32[1,128]{1,0:T(1,128)}, u32[]{:S(2)}) copy-start(f32[1,128]{1,0:T(1,128)} %constant.37.clone.freq_ref) | copy-start | bytes 1540
  30.5 24.2 %collective-permute-start.7 = (bf16[3,160,512]{2,1,0:T(8,128)(2,1)S(1)}, bf16[3,160,512]{2,1,0:T(8,128)(2,1)S(1)}, u32[]{:S(2)}, u32[]{:S(2)}) collective-permute-start(bf16[3,160,512]{2,1,0:T(8,128)(2,1)S(1)} %pad_maximum_fusion.refs_6_.refs_3_), channel_id=1, source_target_pairs={{0,64},{64,128},{128,192},{192,0},{1,65},{65,129},{129,193},{193,1... | collective-permute-start | bytes 1474568 | tf_op jit(solution)/shard_map/ppermute | solution.py:35
  31.0 25.0 %collective-permute-start.8 = (bf16[3,160,512]{2,1,0:T(8,128)(2,1)S(1)}, bf16[3,160,512]{2,1,0:T(8,128)(2,1)S(1)}, u32[]{:S(2)}, u32[]{:S(2)}) collective-permute-start(bf16[3,160,512]{2,1,0:T(8,128)(2,1)S(1)} %pad_maximum_fusion.refs_6_.refs_3_), channel_id=1, source_target_pairs={{0,128},{64,192},{128,0},{192,64},{1,129},{65,193},{129,1},{193,65... | collective-permute-start | bytes 1474568 | tf_op jit(solution)/shard_map/ppermute | solution.py:35
  31.5 26.9 %collective-permute-start.9 = (bf16[3,160,512]{2,1,0:T(8,128)(2,1)S(1)}, bf16[3,160,512]{2,1,0:T(8,128)(2,1)S(1)}, u32[]{:S(2)}, u32[]{:S(2)}) collective-permute-start(bf16[3,160,512]{2,1,0:T(8,128)(2,1)S(1)} %pad_maximum_fusion.refs_6_.refs_3_), channel_id=1, source_target_pairs={{0,192},{64,0},{128,64},{192,128},{1,193},{65,1},{129,65},{193,129... | collective-permute-start | bytes 1474568 | tf_op jit(solution)/shard_map/ppermute | solution.py:35
  33.5 4.8 %collective-permute-start.20 = (bf16[160,512]{1,0:T(8,128)(2,1)S(1)}, bf16[160,512]{1,0:T(8,128)(2,1)S(1)}, u32[]{:S(2)}, u32[]{:S(2)}) collective-permute-start(bf16[160,512]{1,0:T(8,128)(2,1)S(1)} %collective-permute-done.12.refs_12_.refs_9_), channel_id=1, source_target_pairs={{0,1},{1,0},{2,3},{3,2},{4,5},{5,4},{6,7},{7,6},{8,9},{9,8},{10,11... | collective-permute-start | bytes 491528 | tf_op jit(solution)/shard_map/ppermute | solution.py:35
  37.2 2.2 %collective-permute-start.21 = (bf16[160,512]{1,0:T(8,128)(2,1)S(1)}, bf16[160,512]{1,0:T(8,128)(2,1)S(1)}, u32[]{:S(2)}, u32[]{:S(2)}) collective-permute-start(bf16[160,512]{1,0:T(8,128)(2,1)S(1)} %collective-permute-done.13.refs_13_.refs_10_), channel_id=1, source_target_pairs={{0,1},{1,0},{2,3},{3,2},{4,5},{5,4},{6,7},{7,6},{8,9},{9,8},{10,11... | collective-permute-start | bytes 491528 | tf_op jit(solution)/shard_map/ppermute | solution.py:35
  38.3 20.5 %collective-permute-start.3 = (bf16[64,5120]{1,0:T(8,128)(2,1)S(1)}, bf16[64,5120]{1,0:T(8,128)(2,1)S(1)}, u32[]{:S(2)}, u32[]{:S(2)}) collective-permute-start(bf16[64,5120]{1,0:T(8,128)(2,1)S(1)} %get-tuple-element.51), channel_id=1, source_target_pairs={{0,4},{4,8},{8,12},{12,0},{1,5},{5,9},{9,13},{13,1},{2,6},{6,10},{... | collective-permute-start | bytes 1966088 | tf_op jit(solution)/shard_map/ppermute | solution.py:35
  39.5 19.6 %collective-permute-start.2 = (bf16[64,5120]{1,0:T(8,128)(2,1)S(1)}, bf16[64,5120]{1,0:T(8,128)(2,1)S(1)}, u32[]{:S(2)}, u32[]{:S(2)}) collective-permute-start(bf16[64,5120]{1,0:T(8,128)(2,1)S(1)} %get-tuple-element.50), channel_id=1, source_target_pairs={{0,12},{4,0},{8,4},{12,8},{1,13},{5,1},{9,5},{13,9},{2,14},{6,2},{... | collective-permute-start | bytes 1966088 | tf_op jit(solution)/shard_map/ppermute | solution.py:35
  54.6 3.8 %collective-permute-start.14 = (bf16[3,160,512]{2,1,0:T(8,128)(2,1)S(1)}, bf16[3,160,512]{2,1,0:T(8,128)(2,1)S(1)}, u32[]{:S(2)}, u32[]{:S(2)}) collective-permute-start(bf16[3,160,512]{2,1,0:T(8,128)(2,1)S(1)} %pad_maximum_fusion.refs_6_.refs_3_), channel_id=1, source_target_pairs={{0,1},{1,0},{2,3},{3,2},{4,5},{5,4},{6,7},{7,6},{8,9},{9,8},{10,11... | collective-permute-start | bytes 1474568 | tf_op jit(solution)/shard_map/ppermute | solution.py:35
  56.0 16.6 %collective-permute-start.1 = (bf16[64,5120]{1,0:T(8,128)(2,1)S(1)}, bf16[64,5120]{1,0:T(8,128)(2,1)S(1)}, u32[]{:S(2)}, u32[]{:S(2)}) collective-permute-start(bf16[64,5120]{1,0:T(8,128)(2,1)S(1)} %get-tuple-element.51), channel_id=1, source_target_pairs={{0,12},{4,0},{8,4},{12,8},{1,13},{5,1},{9,5},{13,9},{2,14},{6,2},{... | collective-permute-start | bytes 1966088 | tf_op jit(solution)/shard_map/ppermute | solution.py:35
  58.4 17.2 %collective-permute-start.4 = (bf16[64,5120]{1,0:T(8,128)(2,1)S(1)}, bf16[64,5120]{1,0:T(8,128)(2,1)S(1)}, u32[]{:S(2)}, u32[]{:S(2)}) collective-permute-start(bf16[64,5120]{1,0:T(8,128)(2,1)S(1)} %get-tuple-element.50), channel_id=1, source_target_pairs={{0,4},{4,8},{8,12},{12,0},{1,5},{5,9},{9,13},{13,1},{2,6},{6,10},{... | collective-permute-start | bytes 1966088 | tf_op jit(solution)/shard_map/ppermute | solution.py:35
  58.4 19.3 %collective-permute-start.15 = (bf16[3,160,512]{2,1,0:T(8,128)(2,1)S(1)}, bf16[3,160,512]{2,1,0:T(8,128)(2,1)S(1)}, u32[]{:S(2)}, u32[]{:S(2)}) collective-permute-start(bf16[3,160,512]{2,1,0:T(8,128)(2,1)S(1)} %collective-permute-done.7.refs_7_.refs_4_), channel_id=1, source_target_pairs={{0,1},{1,0},{2,3},{3,2},{4,5},{5,4},{6,7},{7,6},{8,9},{9,8},{10,11... | collective-permute-start | bytes 1474568 | tf_op jit(solution)/shard_map/ppermute | solution.py:35
  58.8 18.9 %collective-permute-start.16 = (bf16[3,160,512]{2,1,0:T(8,128)(2,1)S(1)}, bf16[3,160,512]{2,1,0:T(8,128)(2,1)S(1)}, u32[]{:S(2)}, u32[]{:S(2)}) collective-permute-start(bf16[3,160,512]{2,1,0:T(8,128)(2,1)S(1)} %collective-permute-done.8.refs_8_.refs_5_), channel_id=1, source_target_pairs={{0,1},{1,0},{2,3},{3,2},{4,5},{5,4},{6,7},{7,6},{8,9},{9,8},{10,11... | collective-permute-start | bytes 1474568 | tf_op jit(solution)/shard_map/ppermute | solution.py:35
  59.0 18.7 %collective-permute-start.17 = (bf16[3,160,512]{2,1,0:T(8,128)(2,1)S(1)}, bf16[3,160,512]{2,1,0:T(8,128)(2,1)S(1)}, u32[]{:S(2)}, u32[]{:S(2)}) collective-permute-start(bf16[3,160,512]{2,1,0:T(8,128)(2,1)S(1)} %collective-permute-done.9.refs_9_.refs_6_), channel_id=1, source_target_pairs={{0,1},{1,0},{2,3},{3,2},{4,5},{5,4},{6,7},{7,6},{8,9},{9,8},{10,11... | collective-permute-start | bytes 1474568 | tf_op jit(solution)/shard_map/ppermute | solution.py:35
  72.5 19.9 %collective-permute-start.22 = (bf16[64,5120]{1,0:T(8,128)(2,1)S(1)}, bf16[64,5120]{1,0:T(8,128)(2,1)S(1)}, u32[]{:S(2)}, u32[]{:S(2)}) collective-permute-start(bf16[64,5120]{1,0:T(8,128)(2,1)S(1)} %collective-permute-done.3.refs_4_), channel_id=1, source_target_pairs={{0,4},{4,8},{8,12},{12,0},{1,5},{5,9},{9,13},{13,1},{2,6},{6,10},{... | collective-permute-start | bytes 1966088 | tf_op jit(solution)/shard_map/ppermute | solution.py:35
  75.6 16.7 %collective-permute-start.23 = (bf16[64,5120]{1,0:T(8,128)(2,1)S(1)}, bf16[64,5120]{1,0:T(8,128)(2,1)S(1)}, u32[]{:S(2)}, u32[]{:S(2)}) collective-permute-start(bf16[64,5120]{1,0:T(8,128)(2,1)S(1)} %collective-permute-done.2.refs_3_), channel_id=1, source_target_pairs={{0,12},{4,0},{8,4},{12,8},{1,13},{5,1},{9,5},{13,9},{2,14},{6,2},{... | collective-permute-start | bytes 1966088 | tf_op jit(solution)/shard_map/ppermute | solution.py:35
  77.7 3.1 %copy-start.4 = (bf16[1,128,4096]{2,1,0:T(8,128)(2,1)S(1)}, bf16[1,128,4096]{2,1,0:T(8,128)(2,1)}, u32[]{:S(2)}) copy-start(bf16[1,128,4096]{2,1,0:T(8,128)(2,1)} %param.7) | copy-start | bytes 3145732
  80.8 9.6 %collective-permute-start.26 = (bf16[384,512]{1,0:T(8,128)(2,1)S(1)}, bf16[384,512]{1,0:T(8,128)(2,1)S(1)}, u32[]{:S(2)}, u32[]{:S(2)}) collective-permute-start(bf16[384,512]{1,0:T(8,128)(2,1)S(1)} %project.2.refs_5_.refs_6_), channel_id=1, source_target_pairs={{0,2},{2,0},{1,3},{3,1},{4,6},{6,4},{5,7},{7,5},{8,10},{10,8},{9,1... | collective-permute-start | bytes 1179656 | tf_op jit(solution)/shard_map/ppermute | solution.py:35
  81.6 21.0 %copy-start.2 = (s32[1,16]{1,0:T(1,128)S(1)}, s32[1,16]{1,0:T(1,128)}, u32[]{:S(2)}) copy-start(s32[1,16]{1,0:T(1,128)} %refs_2_.5) | copy-start | bytes 196
  81.6 15.0 %collective-permute-start = (bf16[128,1024]{1,0:T(8,128)(2,1)S(1)}, bf16[128,1024]{1,0:T(8,128)(2,1)S(1)}, u32[]{:S(2)}, u32[]{:S(2)}) collective-permute-start(bf16[128,1024]{1,0:T(8,128)(2,1)S(1)} %get-tuple-element.55), channel_id=1, source_target_pairs={{0,8},{4,12},{8,0},{12,4},{1,9},{5,13},{9,1},{13,5},{2,10},{6,14},... | collective-permute-start | bytes 786440 | tf_op jit(solution)/shard_map/ppermute | solution.py:35
  82.9 18.7 %collective-permute-start.24 = (bf16[384,512]{1,0:T(8,128)(2,1)S(1)}, bf16[384,512]{1,0:T(8,128)(2,1)S(1)}, u32[]{:S(2)}, u32[]{:S(2)}) collective-permute-start(bf16[384,512]{1,0:T(8,128)(2,1)S(1)} %project.2.refs_5_.refs_6_), channel_id=1, source_target_pairs={{0,1},{1,0},{2,3},{3,2},{4,5},{5,4},{6,7},{7,6},{8,9},{9,8},{10,11... | collective-permute-start | bytes 1179656 | tf_op jit(solution)/shard_map/ppermute | solution.py:35
  90.4 12.3 %collective-permute-start.28 = (bf16[384,512]{1,0:T(8,128)(2,1)S(1)}, bf16[384,512]{1,0:T(8,128)(2,1)S(1)}, u32[]{:S(2)}, u32[]{:S(2)}) collective-permute-start(bf16[384,512]{1,0:T(8,128)(2,1)S(1)} %collective-permute-done.26.refs_9_.refs_10_), channel_id=1, source_target_pairs={{0,1},{1,0},{2,3},{3,2},{4,5},{5,4},{6,7},{7,6},{8,9},{9,8},{10,11... | collective-permute-start | bytes 1179656 | tf_op jit(solution)/shard_map/ppermute | solution.py:35
  94.2 4.6 %collective-permute-start.27 = (bf16[128,512]{1,0:T(8,128)(2,1)S(1)}, bf16[128,512]{1,0:T(8,128)(2,1)S(1)}, u32[]{:S(2)}, u32[]{:S(2)}) collective-permute-start(bf16[128,512]{1,0:T(8,128)(2,1)S(1)} %project.3.refs_6_.refs_7_), channel_id=1, source_target_pairs={{0,2},{2,0},{1,3},{3,1},{4,6},{6,4},{5,7},{7,5},{8,10},{10,8},{9,1... | collective-permute-start | bytes 393224 | tf_op jit(solution)/shard_map/ppermute | solution.py:35
  94.3 6.2 %collective-permute-start.25 = (bf16[128,512]{1,0:T(8,128)(2,1)S(1)}, bf16[128,512]{1,0:T(8,128)(2,1)S(1)}, u32[]{:S(2)}, u32[]{:S(2)}) collective-permute-start(bf16[128,512]{1,0:T(8,128)(2,1)S(1)} %project.3.refs_6_.refs_7_), channel_id=1, source_target_pairs={{0,1},{1,0},{2,3},{3,2},{4,5},{5,4},{6,7},{7,6},{8,9},{9,8},{10,11... | collective-permute-start | bytes 393224 | tf_op jit(solution)/shard_map/ppermute | solution.py:35
  96.7 8.1 %collective-permute-start.30 = (bf16[128,1024]{1,0:T(8,128)(2,1)S(1)}, bf16[128,1024]{1,0:T(8,128)(2,1)S(1)}, u32[]{:S(2)}, u32[]{:S(2)}) collective-permute-start(bf16[128,1024]{1,0:T(8,128)(2,1)S(1)} %get-tuple-element.54), channel_id=1, source_target_pairs={{0,12},{4,0},{8,4},{12,8},{1,13},{5,1},{9,5},{13,9},{2,14},{6,2},{... | collective-permute-start | bytes 786440 | tf_op jit(solution)/shard_map/ppermute | solution.py:35
  98.8 6.4 %collective-permute-start.31 = (bf16[128,1024]{1,0:T(8,128)(2,1)S(1)}, bf16[128,1024]{1,0:T(8,128)(2,1)S(1)}, u32[]{:S(2)}, u32[]{:S(2)}) collective-permute-start(bf16[128,1024]{1,0:T(8,128)(2,1)S(1)} %get-tuple-element.53), channel_id=1, source_target_pairs={{0,4},{4,8},{8,12},{12,0},{1,5},{5,9},{9,13},{13,1},{2,6},{6,10},{... | collective-permute-start | bytes 786440 | tf_op jit(solution)/shard_map/ppermute | solution.py:35
  100.5 2.2 %collective-permute-start.29 = (bf16[128,512]{1,0:T(8,128)(2,1)S(1)}, bf16[128,512]{1,0:T(8,128)(2,1)S(1)}, u32[]{:S(2)}, u32[]{:S(2)}) collective-permute-start(bf16[128,512]{1,0:T(8,128)(2,1)S(1)} %collective-permute-done.27.refs_10_.refs_11_), channel_id=1, source_target_pairs={{0,1},{1,0},{2,3},{3,2},{4,5},{5,4},{6,7},{7,6},{8,9},{9,8},{10,11... | collective-permute-start | bytes 393224 | tf_op jit(solution)/shard_map/ppermute | solution.py:35
  111.8 8.9 %collective-permute-start.35 = (f32[2,16,256]{2,1,0:T(8,128)S(1)}, f32[2,16,256]{2,1,0:T(8,128)S(1)}, u32[]{:S(2)}, u32[]{:S(2)}) collective-permute-start(f32[2,16,256]{2,1,0:T(8,128)S(1)} %dynamic-slice_bitcast_fusion), channel_id=1, source_target_pairs={{0,1},{1,0},{2,3},{3,2},{4,5},{5,4},{6,7},{7,6},{8,9},{9,8},{10,11... | collective-permute-start | bytes 98312 | tf_op jit(solution)/shard_map/ppermute | solution.py:35
  116.2 8.8 %collective-permute-start.32 = (bf16[128,1024]{1,0:T(8,128)(2,1)S(1)}, bf16[128,1024]{1,0:T(8,128)(2,1)S(1)}, u32[]{:S(2)}, u32[]{:S(2)}) collective-permute-start(bf16[128,1024]{1,0:T(8,128)(2,1)S(1)} %get-tuple-element.40), channel_id=1, source_target_pairs={{0,12},{4,0},{8,4},{12,8},{1,13},{5,1},{9,5},{13,9},{2,14},{6,2},{... | collective-permute-start | bytes 786440 | tf_op jit(solution)/shard_map/ppermute | solution.py:35
  117.5 8.7 %collective-permute-start.34 = (bf16[128,1024]{1,0:T(8,128)(2,1)S(1)}, bf16[128,1024]{1,0:T(8,128)(2,1)S(1)}, u32[]{:S(2)}, u32[]{:S(2)}) collective-permute-start(bf16[128,1024]{1,0:T(8,128)(2,1)S(1)} %get-tuple-element.42), channel_id=1, source_target_pairs={{0,4},{4,8},{8,12},{12,0},{1,5},{5,9},{9,13},{13,1},{2,6},{6,10},{... | collective-permute-start | bytes 786440 | tf_op jit(solution)/shard_map/ppermute | solution.py:35
  118.4 14.0 %collective-permute-start.33 = (bf16[128,1024]{1,0:T(8,128)(2,1)S(1)}, bf16[128,1024]{1,0:T(8,128)(2,1)S(1)}, u32[]{:S(2)}, u32[]{:S(2)}) collective-permute-start(bf16[128,1024]{1,0:T(8,128)(2,1)S(1)} %get-tuple-element.41), channel_id=1, source_target_pairs={{0,8},{4,12},{8,0},{12,4},{1,9},{5,13},{9,1},{13,5},{2,10},{6,14},... | collective-permute-start | bytes 786440 | tf_op jit(solution)/shard_map/ppermute | solution.py:35
  120.8 3.0 %collective-permute-start.36 = (f32[16,256]{1,0:T(8,128)S(1)}, f32[16,256]{1,0:T(8,128)S(1)}, u32[]{:S(2)}, u32[]{:S(2)}) collective-permute-start(f32[16,256]{1,0:T(8,128)S(1)} %dynamic-slice_bitcast_fusion.1), channel_id=1, source_target_pairs={{0,2},{2,0},{1,3},{3,1},{4,6},{6,4},{5,7},{7,5},{8,10},{10,8},{9,1... | collective-permute-start | bytes 49160 | tf_op jit(solution)/shard_map/ppermute | solution.py:35

commit v2 on v1

--- a/solution.py
+++ b/solution.py
@@ -85,15 +85,16 @@
 
 def proj_kernel(n, first, *refs):
     idx, hs, refs = refs[0], refs[1 : 1 + n], refs[1 + n :]
-    sets, refs = (refs[:8], refs[8:16]), refs[16:]
+    sets, refs = (refs[:10], refs[10:20]), refs[20:]
     cos_ref, sin_ref, out_ref, wbuf, acc = refs
     core, zh, my_y = idx[2], idx[3], idx[4]
     span = 4 * ROWS
     for d in range(4):
         for m, c in enumerate((core, 1 - core)):
-            for r, turn in enumerate((0, 3, 1)):
-                wbuf[d, lax.rem(zh + turn, 4), c] = sets[m][d][r]
-            wbuf[d, lax.rem(zh + 2, 4), c] = sets[m][4 + d][...]
+            for r, turn in enumerate((0, 3, 1, 2)):
+                group, part = sets[m][r // 2 * 5 : r // 2 * 5 + 5], r % 2
+                piece = group[3 + part][...] if d == 2 else group[(0, 1, 0, 2)[d]][part]
+                wbuf[d, lax.rem(zh + turn, 4), c] = piece
         start = pl.multiple_of(lax.rem(my_y + 4 - d, 4) * span, HEAD)
         h = jnp.concatenate([ref[:, pl.ds(start, span)] for ref in hs], axis=0)
         p = jnp.dot(h, wbuf[d].reshape(span, COLS), preferred_element_type=F32)
@@ -117,7 +118,7 @@
     return pl.pallas_call(
         functools.partial(proj_kernel, len(pieces), first),
         out_shape=jax.ShapeDtypeStruct((row, COLS), BF),
-        in_specs=[pl.BlockSpec(memory_space=pltpu.SMEM)] + [vm] * (len(pieces) + 18),
+        in_specs=[pl.BlockSpec(memory_space=pltpu.SMEM)] + [vm] * (len(pieces) + 22),
         out_specs=vm,
         scratch_shapes=[
             pltpu.VMEM((4, 4, 2, HALF, COLS), BF),
@@ -186,8 +187,9 @@
 
         def values(i, carry, lo=lo):
             base = pl.multiple_of((lo + 2 * i) * TOK, TOK)
-            for e in range(2):
-                v = kvbuf[pl.ds(base, CHUNK), 256 + e * HEAD : 256 + (e + 1) * HEAD]
+
+            def one_head(e, inner):
+                v = kvbuf[pl.ds(base, CHUNK), pl.ds(pl.multiple_of(256 + e * HEAD, HEAD), HEAD)]
                 for g in range(4):
                     r = slice(g * TOK, (g + 1) * TOK)
                     peak = mx[e, r]
@@ -196,7 +198,9 @@
                     ls[e, r] = ls[e, r] + (p0 + p1)
                     p = jnp.concatenate([p0.astype(BF), p1.astype(BF)], axis=1)
                     acc[e, r] = acc[e, r] + jnp.dot(p, v, preferred_element_type=F32)
-            return carry
+                return inner
+
+            return lax.fori_loop(0, 2, one_head, carry)
 
         lax.fori_loop(0, n_chunks, values, 0)
         for e in range(2):
@@ -277,7 +281,6 @@
     vals = lax.dynamic_slice(weight, (row_at, value_at), (HALF, 256))
     own = jnp.concatenate([keys, vals], axis=1)
     z1 = shift(own, "zh", 1)
-    z3 = shift(own, "zh", -1)
     half = TOK // 2
     top, bottom = h[:half], h[half:]
     top_left = shift(top, "x", 1)
@@ -286,14 +289,20 @@
     top_right = shift(top, "x", -1)
     far_top = shift(top_left, "x", 1)
     far_bottom = shift(bottom_right, "x", -1)
-    z2 = shift(own, "zh", 2)
-    three = jnp.stack([own, z1, z3])
-    mine = [three] + [None] * 3 + [z2] + [None] * 3
-    for d in (1, 3, 2):
-        mine[d] = shift(three, "y", d)
-    for d in (1, 3, 2):
-        mine[4 + d] = shift(z2, "y", d)
-    weights = mine + [shift(v, "c", 1) for v in mine]
+    z3 = shift(own, "zh", -1)
+    z2 = shift(z1, "zh", 1)
+    first, last = jnp.stack([own, z1]), jnp.stack([z3, z2])
+    mine = []
+    for both in (first, last):
+        one = shift(both, "y", 1)
+        three = shift(both, "y", -1)
+        far0 = shift(one[0], "y", 1)
+        far1 = shift(three[1], "y", -1)
+        mine += [both, one, three, far0, far1]
+    theirs = []
+    for v in mine:
+        theirs.append(shift(v, "c", 1))
+    weights = mine + theirs
 
     gives = [lax.dynamic_slice(q, (jnp.uint32(0), at), (TOK, OCOLS)) for at in spots]
     q1 = shift(gives[3], "x", -1)

time: 134 us -> 140 us (1.045)
  the two profiles are of different devices: /device:TPU:1 before, /device:TPU:8 now
where the time goes in v2:
time: 140 us; the launch traced here: 137 us
  waiting for transfers between devices  73.6 us (53%)
  starting transfers between devices  39.6 us (28%)
  Pallas kernels  20.1 us (14%)
  local copies, waits for them, and re-layouts  2.13 us (2%)
    ppermute x41, waiting for transfers between devices, shift(): return lax.ppermute(v, axis, [(i, (i + d) % n) for i in range(n)])  73.6 us
    ppermute x41, starting transfers between devices, shift(): return lax.ppermute(v, axis, [(i, (i + d) % n) for i in range(n)])  39.6 us
    pallas_call x3, Pallas kernels, attend(): pl.pallas_call(functools.partial(attn_kernel, js), out_shape=[jax.ShapeDt...  11.9 us
    pallas_call x2, Pallas kernels, project(): pl.pallas_call(functools.partial(proj_kernel, len(pieces), first), out_sh...  4.81 us
  transfers between devices with their start and end apart: 41, of which 19 were waited for; matrix products, arithmetic and copies ran while one was open for 1% of the time, Pallas kernels for 8%

profile of v2, /device:TPU:8, one launch (start us, length us, event | category | flops | bytes accessed | tf_op | source)
XLA Modules:
  0.0 137.2 jit_solution(9280861280082746324)
XLA Ops:
  0.7 1.1 fusion.3
  1.9 3.3 %collective-permute-start.5 = (bf16[160,512]{1,0:T(8,128)(2,1)S(1)}, bf16[160,512]{1,0:T(8,128)(2,1)S(1)}, u32[]{:S(2)}, u32[]{:S(2)}) collective-permute-start(bf16[160,512]{1,0:T(8,128)(2,1)S(1)} %get-tuple-element.57), channel_id=1, source_target_pairs={{0,16},{16,32},{32,48},{48,0},{1,17},{17,33},{33,49},{49,1},{2,18}... | collective-permute-start | bytes 491528 | tf_op jit(solution)/shard_map/ppermute | solution.py:35
  5.2 8.4 %collective-permute-done.5 = bf16[160,512]{1,0:T(8,128)(2,1)S(1)} collective-permute-done((bf16[160,512]{1,0:T(8,128)(2,1)S(1)}, bf16[160,512]{1,0:T(8,128)(2,1)S(1)}, u32[]{:S(2)}, u32[]{:S(2)}) %collective-permute-start.5) | collective-permute-done | bytes 163872 | tf_op jit(solution)/shard_map/ppermute | solution.py:35
  13.7 1.7 %collective-permute-start.6 = (bf16[2,160,512]{2,1,0:T(8,128)(2,1)S(1)}, bf16[2,160,512]{2,1,0:T(8,128)(2,1)S(1)}, u32[]{:S(2)}, u32[]{:S(2)}) collective-permute-start(bf16[2,160,512]{2,1,0:T(8,128)(2,1)S(1)} %pad_maximum_fusion.refs_6_.refs_3_), channel_id=1, source_target_pairs={{0,64},{64,128},{128,192},{192,0},{1,65},{65,129},{129,193},{193,1... | collective-permute-start | bytes 983048 | tf_op jit(solution)/shard_map/ppermute | solution.py:35
  15.3 5.0 %collective-permute-start.10 = (bf16[160,512]{1,0:T(8,128)(2,1)S(1)}, bf16[160,512]{1,0:T(8,128)(2,1)S(1)}, u32[]{:S(2)}, u32[]{:S(2)}) collective-permute-start(bf16[160,512]{1,0:T(8,128)(2,1)S(1)} %get-tuple-element.57), channel_id=1, source_target_pairs={{0,48},{16,0},{32,16},{48,32},{1,49},{17,1},{33,17},{49,33},{2,50}... | collective-permute-start | bytes 491528 | tf_op jit(solution)/shard_map/ppermute | solution.py:35
  20.3 0.4 collective-permute-start.7
  20.8 4.6 %collective-permute-done.10 = bf16[160,512]{1,0:T(8,128)(2,1)S(1)} collective-permute-done((bf16[160,512]{1,0:T(8,128)(2,1)S(1)}, bf16[160,512]{1,0:T(8,128)(2,1)S(1)}, u32[]{:S(2)}, u32[]{:S(2)}) %collective-permute-start.10) | collective-permute-done | bytes 163872 | tf_op jit(solution)/shard_map/ppermute | solution.py:35
  25.4 4.0 %collective-permute-done.11 = bf16[160,512]{1,0:T(8,128)(2,1)S(1)} collective-permute-done((bf16[160,512]{1,0:T(8,128)(2,1)S(1)}, bf16[160,512]{1,0:T(8,128)(2,1)S(1)}, u32[]{:S(2)}, u32[]{:S(2)}) %collective-permute-start.11) | collective-permute-done | bytes 163872 | tf_op jit(solution)/shard_map/ppermute | solution.py:35
  29.5 1.4 collective-permute-start.12
  30.8 0.7 collective-permute-start.13
  31.6 1.4 collective-permute-start.8
  33.0 0.8 collective-permute-start.9
  33.9 1.6 %collective-permute-start.3 = (bf16[64,5120]{1,0:T(8,128)(2,1)S(1)}, bf16[64,5120]{1,0:T(8,128)(2,1)S(1)}, u32[]{:S(2)}, u32[]{:S(2)}) collective-permute-start(bf16[64,5120]{1,0:T(8,128)(2,1)S(1)} %get-tuple-element.51), channel_id=1, source_target_pairs={{0,4},{4,8},{8,12},{12,0},{1,5},{5,9},{9,13},{13,1},{2,6},{6,10},{... | collective-permute-start | bytes 1966088 | tf_op jit(solution)/shard_map/ppermute | solution.py:35
  35.5 4.6 %collective-permute-done.12.refs_12_.refs_9_ = bf16[2,160,512]{2,1,0:T(8,128)(2,1)S(1)} collective-permute-done((bf16[2,160,512]{2,1,0:T(8,128)(2,1)S(1)}, bf16[2,160,512]{2,1,0:T(8,128)(2,1)S(1)}, u32[]{:S(2)}, u32[]{:S(2)}) %collective-permute-start.12) | collective-permute-done | bytes 327712 | tf_op jit(solution)/shard_map/ppermute | solution.py:35
  40.1 2.7 %collective-permute-start.2 = (bf16[64,5120]{1,0:T(8,128)(2,1)S(1)}, bf16[64,5120]{1,0:T(8,128)(2,1)S(1)}, u32[]{:S(2)}, u32[]{:S(2)}) collective-permute-start(bf16[64,5120]{1,0:T(8,128)(2,1)S(1)} %get-tuple-element.50), channel_id=1, source_target_pairs={{0,12},{4,0},{8,4},{12,8},{1,13},{5,1},{9,5},{13,9},{2,14},{6,2},{... | collective-permute-start | bytes 1966088 | tf_op jit(solution)/shard_map/ppermute | solution.py:35
  42.9 1.3 collective-permute-start.1
  44.2 0.8 collective-permute-start.4
  45.0 0.8 collective-permute-done.21.refs_21_.refs_18_
  45.8 0.8 collective-permute-start.14
  46.6 5.6 %collective-permute-done.3.refs_4_ = bf16[64,5120]{1,0:T(8,128)(2,1)S(1)} collective-permute-done((bf16[64,5120]{1,0:T(8,128)(2,1)S(1)}, bf16[64,5120]{1,0:T(8,128)(2,1)S(1)}, u32[]{:S(2)}, u32[]{:S(2)}) %collective-permute-start.3) | collective-permute-done | bytes 655392 | tf_op jit(solution)/shard_map/ppermute | solution.py:35
  52.3 5.7 %collective-permute-done.2.refs_3_ = bf16[64,5120]{1,0:T(8,128)(2,1)S(1)} collective-permute-done((bf16[64,5120]{1,0:T(8,128)(2,1)S(1)}, bf16[64,5120]{1,0:T(8,128)(2,1)S(1)}, u32[]{:S(2)}, u32[]{:S(2)}) %collective-permute-start.2) | collective-permute-done | bytes 655392 | tf_op jit(solution)/shard_map/ppermute | solution.py:35
  58.0 1.7 %collective-permute-start.15 = (bf16[160,512]{1,0:T(8,128)(2,1)S(1)}, bf16[160,512]{1,0:T(8,128)(2,1)S(1)}, u32[]{:S(2)}, u32[]{:S(2)}) collective-permute-start(bf16[160,512]{1,0:T(8,128)(2,1)S(1)} %slice_bitcast_fusion.2), channel_id=1, source_target_pairs={{0,192},{64,0},{128,64},{192,128},{1,193},{65,1},{129,65},{193,129... | collective-permute-start | bytes 491528 | tf_op jit(solution)/shard_map/ppermute | solution.py:35
  59.6 8.9 %collective-permute-done.1.refs_2_ = bf16[64,5120]{1,0:T(8,128)(2,1)S(1)} collective-permute-done((bf16[64,5120]{1,0:T(8,128)(2,1)S(1)}, bf16[64,5120]{1,0:T(8,128)(2,1)S(1)}, u32[]{:S(2)}, u32[]{:S(2)}) %collective-permute-start.1) | collective-permute-done | bytes 655392 | tf_op jit(solution)/shard_map/ppermute | solution.py:35
  68.6 0.5 collective-permute-start.18
  70.1 0.6 collective-permute-done.20.refs_20_.refs_17_
  71.2 1.2 collective-permute-start.26
  72.4 3.3 %collective-permute-start.27 = (bf16[64,5120]{1,0:T(8,128)(2,1)S(1)}, bf16[64,5120]{1,0:T(8,128)(2,1)S(1)}, u32[]{:S(2)}, u32[]{:S(2)}) collective-permute-start(bf16[64,5120]{1,0:T(8,128)(2,1)S(1)} %collective-permute-done.2.refs_3_), channel_id=1, source_target_pairs={{0,12},{4,0},{8,4},{12,8},{1,13},{5,1},{9,5},{13,9},{2,14},{6,2},{... | collective-permute-start | bytes 1966088 | tf_op jit(solution)/shard_map/ppermute | solution.py:35
  75.7 1.8 %tables.1 = (f32[512,128]{1,0:T(8,128)S(1)}, f32[512,128]{1,0:T(8,128)S(1)}) custom-call(s32[5]{0:T(128)S(1)} %stack.41.idx.refs_0_, s32[1,16]{1,0:T(1,128)S(1)} %copy-done.1, f32[1,128]{1,0:T(1,128)S(1)} %copy-done.3), custom_call_target="tpu_custom_call" | custom-call | flops 4194304 | bytes 1048576 | tf_op jit(solution)/shard_map/tables/pallas_call | solution.py:75
  77.6 3.0 %project.2.refs_5_.refs_6_ = bf16[384,512]{1,0:T(8,128)(2,1)S(1)} custom-call(s32[5]{0:T(128)S(1)} %stack.41.idx.refs_0_, bf16[128,5120]{1,0:T(8,128)(2,1)S(1)} %bitcast.40, bf16[64,5120]{1,0:T(8,128)(2,1)S(1)} %collective-permute-done.1.refs_2_, bf16[64,5120]{1,0:T(8,128)(2,1)S(1)} %collective-permute-done.2.refs_3_, ...), custom_call_target="tpu_custom_call" | custom-call | flops 2013265920 | bytes 18874368 | tf_op jit(solution)/shard_map/project/pallas_call | solution.py:118
  80.8 0.8 constant_dynamic-slice_fusion
  81.5 0.7 collective-permute-start
  82.2 9.4 %collective-permute-done.30.refs_9_.refs_10_ = bf16[384,512]{1,0:T(8,128)(2,1)S(1)} collective-permute-done((bf16[384,512]{1,0:T(8,128)(2,1)S(1)}, bf16[384,512]{1,0:T(8,128)(2,1)S(1)}, u32[]{:S(2)}, u32[]{:S(2)}) %collective-permute-start.30) | collective-permute-done | bytes 393248 | tf_op jit(solution)/shard_map/ppermute | solution.py:35
  91.7 4.1 %collective-permute-done.27.refs_2_ = bf16[64,5120]{1,0:T(8,128)(2,1)S(1)} collective-permute-done((bf16[64,5120]{1,0:T(8,128)(2,1)S(1)}, bf16[64,5120]{1,0:T(8,128)(2,1)S(1)}, u32[]{:S(2)}, u32[]{:S(2)}) %collective-permute-start.27) | collective-permute-done | bytes 655392 | tf_op jit(solution)/shard_map/ppermute | solution.py:35
  95.8 1.8 %project.3.refs_6_.refs_7_ = bf16[128,512]{1,0:T(8,128)(2,1)S(1)} custom-call(s32[5]{0:T(128)S(1)} %stack.41.idx.refs_0_, bf16[64,5120]{1,0:T(8,128)(2,1)S(1)} %collective-permute-done.26.refs_1_, bf16[64,5120]{1,0:T(8,128)(2,1)S(1)} %collective-permute-done.27.refs_2_, bf16[2,160,512]{2,1,0:T(8,128)(2,1)S(1)} %pad_maximum_fusion.refs_6_.refs_3_, ...), custom_call_target="tpu_custom_call" | custom-call | flops 671088640 | bytes 18874368 | tf_op jit(solution)/shard_map/project/pallas_call | solution.py:118
  97.7 3.8 %collective-permute-start.34 = (bf16[128,1024]{1,0:T(8,128)(2,1)S(1)}, bf16[128,1024]{1,0:T(8,128)(2,1)S(1)}, u32[]{:S(2)}, u32[]{:S(2)}) collective-permute-start(bf16[128,1024]{1,0:T(8,128)(2,1)S(1)} %get-tuple-element.54), channel_id=1, source_target_pairs={{0,12},{4,0},{8,4},{12,8},{1,13},{5,1},{9,5},{13,9},{2,14},{6,2},{... | collective-permute-start | bytes 786440 | tf_op jit(solution)/shard_map/ppermute | solution.py:35
  101.6 1.1 collective-permute-done.31.refs_10_.refs_11_
  103.0 1.1 collective-permute-done.33.refs_12_.refs_13_
  104.1 4.6 %attend.3 = (bf16[128,1024]{1,0:T(8,128)(2,1)S(1)}, f32[2,2,16,256]{3,2,1,0:T(8,128)S(1)}) custom-call(s32[5]{0:T(128)S(1)} %stack.41.idx.refs_0_, s32[1,16]{1,0:T(1,128)S(1)} %copy-done.1, s32[1,16]{1,0:T(1,128)S(1)} %copy-done.2, f32[2,2,16,256]{3,2,1,0:T(8,128)S(1)} %broadcast_in_dim.7.refs_3_, bf16[128,1024]{1,0:T(8,128)(2,1)S(1)} %collective-permute-done.refs_4_, ...), custom_call_target="tpu_custom_call" | custom-call | flops 367001600 | bytes 12582912 | tf_op jit(solution)/shard_map/attend/pallas_call | solution.py:228
  108.6 1.4 %collective-permute-done.35.refs_5_ = bf16[128,1024]{1,0:T(8,128)(2,1)S(1)} collective-permute-done((bf16[128,1024]{1,0:T(8,128)(2,1)S(1)}, bf16[128,1024]{1,0:T(8,128)(2,1)S(1)}, u32[]{:S(2)}, u32[]{:S(2)}) %collective-permute-start.35) | collective-permute-done | bytes 262176 | tf_op jit(solution)/shard_map/ppermute | solution.py:35
  110.1 5.1 %attend.4 = (bf16[128,1024]{1,0:T(8,128)(2,1)S(1)}, bf16[128,1024]{1,0:T(8,128)(2,1)S(1)}, f32[2,2,16,256]{3,2,1,0:T(8,128)S(1)}) custom-call(s32[5]{0:T(128)S(1)} %stack.41.idx.refs_0_, s32[1,16]{1,0:T(1,128)S(1)} %copy-done.1, s32[1,16]{1,0:T(1,128)S(1)} %copy-done.2, f32[2,2,16,256]{3,2,1,0:T(8,128)S(1)} %get-tuple-element.34.refs_3_, ...), custom_call_target="tpu_custom_call" | custom-call | flops 734003200 | bytes 25165824 | tf_op jit(solution)/shard_map/attend/pallas_call | solution.py:228
  115.2 2.2 %attend.5 = (bf16[128,1024]{1,0:T(8,128)(2,1)S(1)}, f32[2,2,16,256]{3,2,1,0:T(8,128)S(1)}) custom-call(s32[5]{0:T(128)S(1)} %stack.41.idx.refs_0_, s32[1,16]{1,0:T(1,128)S(1)} %copy-done.1, s32[1,16]{1,0:T(1,128)S(1)} %copy-done.2, f32[2,2,16,256]{3,2,1,0:T(8,128)S(1)} %get-tuple-element.37.refs_3_, bf16[128,1024]{1,0:T(8,128)(2,1)S(1)} %get-tuple-element.52.refs_4_, ...), custom_call_target="tpu_custom_call" | custom-call | flops 367001600 | bytes 12582912 | tf_op jit(solution)/shard_map/attend/pallas_call | solution.py:228
  117.6 3.2 %collective-permute-start.36 = (bf16[128,1024]{1,0:T(8,128)(2,1)S(1)}, bf16[128,1024]{1,0:T(8,128)(2,1)S(1)}, u32[]{:S(2)}, u32[]{:S(2)}) collective-permute-start(bf16[128,1024]{1,0:T(8,128)(2,1)S(1)} %get-tuple-element.40), channel_id=1, source_target_pairs={{0,12},{4,0},{8,4},{12,8},{1,13},{5,1},{9,5},{13,9},{2,14},{6,2},{... | collective-permute-start | bytes 786440 | tf_op jit(solution)/shard_map/ppermute | solution.py:35
  120.8 1.5 %collective-permute-start.37 = (bf16[128,1024]{1,0:T(8,128)(2,1)S(1)}, bf16[128,1024]{1,0:T(8,128)(2,1)S(1)}, u32[]{:S(2)}, u32[]{:S(2)}) collective-permute-start(bf16[128,1024]{1,0:T(8,128)(2,1)S(1)} %get-tuple-element.41), channel_id=1, source_target_pairs={{0,8},{4,12},{8,0},{12,4},{1,9},{5,13},{9,1},{13,5},{2,10},{6,14},... | collective-permute-start | bytes 786440 | tf_op jit(solution)/shard_map/ppermute | solution.py:35
  122.4 3.7 %collective-permute-done.40 = f32[16,256]{1,0:T(8,128)S(1)} collective-permute-done((f32[16,256]{1,0:T(8,128)S(1)}, f32[16,256]{1,0:T(8,128)S(1)}, u32[]{:S(2)}, u32[]{:S(2)}) %collective-permute-start.40) | collective-permute-done | bytes 16416 | tf_op jit(solution)/shard_map/ppermute | solution.py:35
  126.1 0.7 fusion.1
  126.8 5.4 %collective-permute-done.36.refs_1_ = bf16[128,1024]{1,0:T(8,128)(2,1)S(1)} collective-permute-done((bf16[128,1024]{1,0:T(8,128)(2,1)S(1)}, bf16[128,1024]{1,0:T(8,128)(2,1)S(1)}, u32[]{:S(2)}, u32[]{:S(2)}) %collective-permute-start.36) | collective-permute-done | bytes 262176 | tf_op jit(solution)/shard_map/ppermute | solution.py:35
  132.2 3.4 %collective-permute-done.38.refs_3_ = bf16[128,1024]{1,0:T(8,128)(2,1)S(1)} collective-permute-done((bf16[128,1024]{1,0:T(8,128)(2,1)S(1)}, bf16[128,1024]{1,0:T(8,128)(2,1)S(1)}, u32[]{:S(2)}, u32[]{:S(2)}) %collective-permute-start.38) | collective-permute-done | bytes 262176 | tf_op jit(solution)/shard_map/ppermute | solution.py:35
  135.6 1.6 %assemble.1 = bf16[1,128,4096]{2,1,0:T(8,128)(2,1)} custom-call(s32[5]{0:T(128)S(1)} %stack.41.idx.refs_0_, bf16[128,1024]{1,0:T(8,128)(2,1)S(1)} %get-tuple-element.39.refs_0_, bf16[128,1024]{1,0:T(8,128)(2,1)S(1)} %collective-permute-done.36.refs_1_, bf16[128,1024]{1,0:T(8,128)(2,1)S(1)} %collective-permute-done.37.refs_2_, ...), custom_call_target="tpu_custom_call" | custom-call | bytes 2097152 | tf_op jit(solution)/shard_map/assemble/pallas_call | solution.py:259
  (68 shorter events, 2.8 us)
Async XLA Ops:
  1.8 32.0 %copy-start = (bf16[1,128,5120]{2,1,0:T(8,128)(2,1)S(1)}, bf16[1,128,5120]{2,1,0:T(8,128)(2,1)}, u32[]{:S(2)}) copy-start(bf16[1,128,5120]{2,1,0:T(8,128)(2,1)} %param.6) | copy-start | bytes 3932164
  1.9 11.8 %collective-permute-start.5 = (bf16[160,512]{1,0:T(8,128)(2,1)S(1)}, bf16[160,512]{1,0:T(8,128)(2,1)S(1)}, u32[]{:S(2)}, u32[]{:S(2)}) collective-permute-start(bf16[160,512]{1,0:T(8,128)(2,1)S(1)} %get-tuple-element.57), channel_id=1, source_target_pairs={{0,16},{16,32},{32,48},{48,0},{1,17},{17,33},{33,49},{49,1},{2,18}... | collective-permute-start | bytes 491528 | tf_op jit(solution)/shard_map/ppermute | solution.py:35
  13.7 17.9 %collective-permute-start.6 = (bf16[2,160,512]{2,1,0:T(8,128)(2,1)S(1)}, bf16[2,160,512]{2,1,0:T(8,128)(2,1)S(1)}, u32[]{:S(2)}, u32[]{:S(2)}) collective-permute-start(bf16[2,160,512]{2,1,0:T(8,128)(2,1)S(1)} %pad_maximum_fusion.refs_6_.refs_3_), channel_id=1, source_target_pairs={{0,64},{64,128},{128,192},{192,0},{1,65},{65,129},{129,193},{193,1... | collective-permute-start | bytes 983048 | tf_op jit(solution)/shard_map/ppermute | solution.py:35
  15.3 10.1 %collective-permute-start.10 = (bf16[160,512]{1,0:T(8,128)(2,1)S(1)}, bf16[160,512]{1,0:T(8,128)(2,1)S(1)}, u32[]{:S(2)}, u32[]{:S(2)}) collective-permute-start(bf16[160,512]{1,0:T(8,128)(2,1)S(1)} %get-tuple-element.57), channel_id=1, source_target_pairs={{0,48},{16,0},{32,16},{48,32},{1,49},{17,1},{33,17},{49,33},{2,50}... | collective-permute-start | bytes 491528 | tf_op jit(solution)/shard_map/ppermute | solution.py:35
  20.3 9.1 %collective-permute-start.11 = (bf16[160,512]{1,0:T(8,128)(2,1)S(1)}, bf16[160,512]{1,0:T(8,128)(2,1)S(1)}, u32[]{:S(2)}, u32[]{:S(2)}) collective-permute-start(bf16[160,512]{1,0:T(8,128)(2,1)S(1)} %collective-permute-done.5), channel_id=1, source_target_pairs={{0,16},{16,32},{32,48},{48,0},{1,17},{17,33},{33,49},{49,1},{2,18}... | collective-permute-start | bytes 491528 | tf_op jit(solution)/shard_map/ppermute | solution.py:35
  20.3 12.6 %collective-permute-start.7 = (bf16[2,160,512]{2,1,0:T(8,128)(2,1)S(1)}, bf16[2,160,512]{2,1,0:T(8,128)(2,1)S(1)}, u32[]{:S(2)}, u32[]{:S(2)}) collective-permute-start(bf16[2,160,512]{2,1,0:T(8,128)(2,1)S(1)} %pad_maximum_fusion.refs_6_.refs_3_), channel_id=1, source_target_pairs={{0,192},{64,0},{128,64},{192,128},{1,193},{65,1},{129,65},{193,129... | collective-permute-start | bytes 983048 | tf_op jit(solution)/shard_map/ppermute | solution.py:35
  20.8 13.1 %collective-permute-start.16 = (bf16[2,160,512]{2,1,0:T(8,128)(2,1)S(1)}, bf16[2,160,512]{2,1,0:T(8,128)(2,1)S(1)}, u32[]{:S(2)}, u32[]{:S(2)}) collective-permute-start(bf16[2,160,512]{2,1,0:T(8,128)(2,1)S(1)} %pad_maximum_fusion.refs_6_.refs_3_), channel_id=1, source_target_pairs={{0,1},{1,0},{2,3},{3,2},{4,5},{5,4},{6,7},{7,6},{8,9},{9,8},{10,11... | collective-permute-start | bytes 983048 | tf_op jit(solution)/shard_map/ppermute | solution.py:35
  29.5 10.7 %collective-permute-start.12 = (bf16[2,160,512]{2,1,0:T(8,128)(2,1)S(1)}, bf16[2,160,512]{2,1,0:T(8,128)(2,1)S(1)}, u32[]{:S(2)}, u32[]{:S(2)}) collective-permute-start(bf16[2,160,512]{2,1,0:T(8,128)(2,1)S(1)} %pad_maximum_fusion.1.refs_11_.refs_8_), channel_id=1, source_target_pairs={{0,64},{64,128},{128,192},{192,0},{1,65},{65,129},{129,193},{193,1... | collective-permute-start | bytes 983048 | tf_op jit(solution)/shard_map/ppermute | solution.py:35
  30.8 12.0 %collective-permute-start.13 = (bf16[2,160,512]{2,1,0:T(8,128)(2,1)S(1)}, bf16[2,160,512]{2,1,0:T(8,128)(2,1)S(1)}, u32[]{:S(2)}, u32[]{:S(2)}) collective-permute-start(bf16[2,160,512]{2,1,0:T(8,128)(2,1)S(1)} %pad_maximum_fusion.1.refs_11_.refs_8_), channel_id=1, source_target_pairs={{0,192},{64,0},{128,64},{192,128},{1,193},{65,1},{129,65},{193,129... | collective-permute-start | bytes 983048 | tf_op jit(solution)/shard_map/ppermute | solution.py:35
  31.6 12.6 %collective-permute-start.8 = (bf16[160,512]{1,0:T(8,128)(2,1)S(1)}, bf16[160,512]{1,0:T(8,128)(2,1)S(1)}, u32[]{:S(2)}, u32[]{:S(2)}) collective-permute-start(bf16[160,512]{1,0:T(8,128)(2,1)S(1)} %slice_bitcast_fusion.5), channel_id=1, source_target_pairs={{0,64},{64,128},{128,192},{192,0},{1,65},{65,129},{129,193},{193,1... | collective-permute-start | bytes 491528 | tf_op jit(solution)/shard_map/ppermute | solution.py:35
  33.0 42.8 %copy-start.1 = (s32[1,16]{1,0:T(1,128)S(1)}, s32[1,16]{1,0:T(1,128)}, u32[]{:S(2)}) copy-start(s32[1,16]{1,0:T(1,128)} %refs_1_.5) | copy-start | bytes 196
  33.0 42.8 %copy-start.3 = (f32[1,128]{1,0:T(1,128)S(1)}, f32[1,128]{1,0:T(1,128)}, u32[]{:S(2)}) copy-start(f32[1,128]{1,0:T(1,128)} %constant.37.clone.freq_ref) | copy-start | bytes 1540
  33.0 11.2 %collective-permute-start.9 = (bf16[160,512]{1,0:T(8,128)(2,1)S(1)}, bf16[160,512]{1,0:T(8,128)(2,1)S(1)}, u32[]{:S(2)}, u32[]{:S(2)}) collective-permute-start(bf16[160,512]{1,0:T(8,128)(2,1)S(1)} %slice_bitcast_fusion.4), channel_id=1, source_target_pairs={{0,192},{64,0},{128,64},{192,128},{1,193},{65,1},{129,65},{193,129... | collective-permute-start | bytes 491528 | tf_op jit(solution)/shard_map/ppermute | solution.py:35
  33.9 18.4 %collective-permute-start.3 = (bf16[64,5120]{1,0:T(8,128)(2,1)S(1)}, bf16[64,5120]{1,0:T(8,128)(2,1)S(1)}, u32[]{:S(2)}, u32[]{:S(2)}) collective-permute-start(bf16[64,5120]{1,0:T(8,128)(2,1)S(1)} %get-tuple-element.51), channel_id=1, source_target_pairs={{0,4},{4,8},{8,12},{12,0},{1,5},{5,9},{9,13},{13,1},{2,6},{6,10},{... | collective-permute-start | bytes 1966088 | tf_op jit(solution)/shard_map/ppermute | solution.py:35
  40.1 17.9 %collective-permute-start.2 = (bf16[64,5120]{1,0:T(8,128)(2,1)S(1)}, bf16[64,5120]{1,0:T(8,128)(2,1)S(1)}, u32[]{:S(2)}, u32[]{:S(2)}) collective-permute-start(bf16[64,5120]{1,0:T(8,128)(2,1)S(1)} %get-tuple-element.50), channel_id=1, source_target_pairs={{0,12},{4,0},{8,4},{12,8},{1,13},{5,1},{9,5},{13,9},{2,14},{6,2},{... | collective-permute-start | bytes 1966088 | tf_op jit(solution)/shard_map/ppermute | solution.py:35
  42.9 25.7 %collective-permute-start.1 = (bf16[64,5120]{1,0:T(8,128)(2,1)S(1)}, bf16[64,5120]{1,0:T(8,128)(2,1)S(1)}, u32[]{:S(2)}, u32[]{:S(2)}) collective-permute-start(bf16[64,5120]{1,0:T(8,128)(2,1)S(1)} %get-tuple-element.51), channel_id=1, source_target_pairs={{0,12},{4,0},{8,4},{12,8},{1,13},{5,1},{9,5},{13,9},{2,14},{6,2},{... | collective-permute-start | bytes 1966088 | tf_op jit(solution)/shard_map/ppermute | solution.py:35
  44.1 1.6 %collective-permute-start.21 = (bf16[2,160,512]{2,1,0:T(8,128)(2,1)S(1)}, bf16[2,160,512]{2,1,0:T(8,128)(2,1)S(1)}, u32[]{:S(2)}, u32[]{:S(2)}) collective-permute-start(bf16[2,160,512]{2,1,0:T(8,128)(2,1)S(1)} %pad_maximum_fusion.1.refs_11_.refs_8_), channel_id=1, source_target_pairs={{0,1},{1,0},{2,3},{3,2},{4,5},{5,4},{6,7},{7,6},{8,9},{9,8},{10,11... | collective-permute-start | bytes 983048 | tf_op jit(solution)/shard_map/ppermute | solution.py:35
  44.2 24.4 %collective-permute-start.4 = (bf16[64,5120]{1,0:T(8,128)(2,1)S(1)}, bf16[64,5120]{1,0:T(8,128)(2,1)S(1)}, u32[]{:S(2)}, u32[]{:S(2)}) collective-permute-start(bf16[64,5120]{1,0:T(8,128)(2,1)S(1)} %get-tuple-element.50), channel_id=1, source_target_pairs={{0,4},{4,8},{8,12},{12,0},{1,5},{5,9},{9,13},{13,1},{2,6},{6,10},{... | collective-permute-start | bytes 1966088 | tf_op jit(solution)/shard_map/ppermute | solution.py:35
  45.8 23.3 %collective-permute-start.14 = (bf16[160,512]{1,0:T(8,128)(2,1)S(1)}, bf16[160,512]{1,0:T(8,128)(2,1)S(1)}, u32[]{:S(2)}, u32[]{:S(2)}) collective-permute-start(bf16[160,512]{1,0:T(8,128)(2,1)S(1)} %slice_bitcast_fusion.3), channel_id=1, source_target_pairs={{0,64},{64,128},{128,192},{192,0},{1,65},{65,129},{129,193},{193,1... | collective-permute-start | bytes 491528 | tf_op jit(solution)/shard_map/ppermute | solution.py:35
  52.3 18.7 %collective-permute-start.17 = (bf16[2,160,512]{2,1,0:T(8,128)(2,1)S(1)}, bf16[2,160,512]{2,1,0:T(8,128)(2,1)S(1)}, u32[]{:S(2)}, u32[]{:S(2)}) collective-permute-start(bf16[2,160,512]{2,1,0:T(8,128)(2,1)S(1)} %collective-permute-done.6.refs_7_.refs_4_), channel_id=1, source_target_pairs={{0,1},{1,0},{2,3},{3,2},{4,5},{5,4},{6,7},{7,6},{8,9},{9,8},{10,11... | collective-permute-start | bytes 983048 | tf_op jit(solution)/shard_map/ppermute | solution.py:35
  58.0 11.2 %collective-permute-start.15 = (bf16[160,512]{1,0:T(8,128)(2,1)S(1)}, bf16[160,512]{1,0:T(8,128)(2,1)S(1)}, u32[]{:S(2)}, u32[]{:S(2)}) collective-permute-start(bf16[160,512]{1,0:T(8,128)(2,1)S(1)} %slice_bitcast_fusion.2), channel_id=1, source_target_pairs={{0,192},{64,0},{128,64},{192,128},{1,193},{65,1},{129,65},{193,129... | collective-permute-start | bytes 491528 | tf_op jit(solution)/shard_map/ppermute | solution.py:35
  68.5 1.4 %collective-permute-start.19 = (bf16[160,512]{1,0:T(8,128)(2,1)S(1)}, bf16[160,512]{1,0:T(8,128)(2,1)S(1)}, u32[]{:S(2)}, u32[]{:S(2)}) collective-permute-start(bf16[160,512]{1,0:T(8,128)(2,1)S(1)} %collective-permute-done.8.refs_9_.refs_6_), channel_id=1, source_target_pairs={{0,1},{1,0},{2,3},{3,2},{4,5},{5,4},{6,7},{7,6},{8,9},{9,8},{10,11... | collective-permute-start | bytes 491528 | tf_op jit(solution)/shard_map/ppermute | solution.py:35
  68.6 2.6 %collective-permute-start.18 = (bf16[2,160,512]{2,1,0:T(8,128)(2,1)S(1)}, bf16[2,160,512]{2,1,0:T(8,128)(2,1)S(1)}, u32[]{:S(2)}, u32[]{:S(2)}) collective-permute-start(bf16[2,160,512]{2,1,0:T(8,128)(2,1)S(1)} %collective-permute-done.7.refs_8_.refs_5_), channel_id=1, source_target_pairs={{0,1},{1,0},{2,3},{3,2},{4,5},{5,4},{6,7},{7,6},{8,9},{9,8},{10,11... | collective-permute-start | bytes 983048 | tf_op jit(solution)/shard_map/ppermute | solution.py:35
  69.1 1.6 %collective-permute-start.20 = (bf16[160,512]{1,0:T(8,128)(2,1)S(1)}, bf16[160,512]{1,0:T(8,128)(2,1)S(1)}, u32[]{:S(2)}, u32[]{:S(2)}) collective-permute-start(bf16[160,512]{1,0:T(8,128)(2,1)S(1)} %collective-permute-done.9.refs_10_.refs_7_), channel_id=1, source_target_pairs={{0,1},{1,0},{2,3},{3,2},{4,5},{5,4},{6,7},{7,6},{8,9},{9,8},{10,11... | collective-permute-start | bytes 491528 | tf_op jit(solution)/shard_map/ppermute | solution.py:35
  69.2 8.4 %collective-permute-start.22 = (bf16[2,160,512]{2,1,0:T(8,128)(2,1)S(1)}, bf16[2,160,512]{2,1,0:T(8,128)(2,1)S(1)}, u32[]{:S(2)}, u32[]{:S(2)}) collective-permute-start(bf16[2,160,512]{2,1,0:T(8,128)(2,1)S(1)} %collective-permute-done.12.refs_12_.refs_9_), channel_id=1, source_target_pairs={{0,1},{1,0},{2,3},{3,2},{4,5},{5,4},{6,7},{7,6},{8,9},{9,8},{10,11... | collective-permute-start | bytes 983048 | tf_op jit(solution)/shard_map/ppermute | solution.py:35
  69.9 7.6 %collective-permute-start.23 = (bf16[2,160,512]{2,1,0:T(8,128)(2,1)S(1)}, bf16[2,160,512]{2,1,0:T(8,128)(2,1)S(1)}, u32[]{:S(2)}, u32[]{:S(2)}) collective-permute-start(bf16[2,160,512]{2,1,0:T(8,128)(2,1)S(1)} %collective-permute-done.13.refs_13_.refs_10_), channel_id=1, source_target_pairs={{0,1},{1,0},{2,3},{3,2},{4,5},{5,4},{6,7},{7,6},{8,9},{9,8},{10,11... | collective-permute-start | bytes 983048 | tf_op jit(solution)/shard_map/ppermute | solution.py:35
  70.6 1.7 %collective-permute-start.24 = (bf16[160,512]{1,0:T(8,128)(2,1)S(1)}, bf16[160,512]{1,0:T(8,128)(2,1)S(1)}, u32[]{:S(2)}, u32[]{:S(2)}) collective-permute-start(bf16[160,512]{1,0:T(8,128)(2,1)S(1)} %collective-permute-done.14.refs_14_.refs_11_), channel_id=1, source_target_pairs={{0,1},{1,0},{2,3},{3,2},{4,5},{5,4},{6,7},{7,6},{8,9},{9,8},{10,11... | collective-permute-start | bytes 491528 | tf_op jit(solution)/shard_map/ppermute | solution.py:35
  70.9 6.6 %collective-permute-start.25 = (bf16[160,512]{1,0:T(8,128)(2,1)S(1)}, bf16[160,512]{1,0:T(8,128)(2,1)S(1)}, u32[]{:S(2)}, u32[]{:S(2)}) collective-permute-start(bf16[160,512]{1,0:T(8,128)(2,1)S(1)} %collective-permute-done.15.refs_15_.refs_12_), channel_id=1, source_target_pairs={{0,1},{1,0},{2,3},{3,2},{4,5},{5,4},{6,7},{7,6},{8,9},{9,8},{10,11... | collective-permute-start | bytes 491528 | tf_op jit(solution)/shard_map/ppermute | solution.py:35
  71.2 20.5 %collective-permute-start.26 = (bf16[64,5120]{1,0:T(8,128)(2,1)S(1)}, bf16[64,5120]{1,0:T(8,128)(2,1)S(1)}, u32[]{:S(2)}, u32[]{:S(2)}) collective-permute-start(bf16[64,5120]{1,0:T(8,128)(2,1)S(1)} %collective-permute-done.3.refs_4_), channel_id=1, source_target_pairs={{0,4},{4,8},{8,12},{12,0},{1,5},{5,9},{9,13},{13,1},{2,6},{6,10},{... | collective-permute-start | bytes 1966088 | tf_op jit(solution)/shard_map/ppermute | solution.py:35
  72.4 23.4 %collective-permute-start.27 = (bf16[64,5120]{1,0:T(8,128)(2,1)S(1)}, bf16[64,5120]{1,0:T(8,128)(2,1)S(1)}, u32[]{:S(2)}, u32[]{:S(2)}) collective-permute-start(bf16[64,5120]{1,0:T(8,128)(2,1)S(1)} %collective-permute-done.2.refs_3_), channel_id=1, source_target_pairs={{0,12},{4,0},{8,4},{12,8},{1,13},{5,1},{9,5},{13,9},{2,14},{6,2},{... | collective-permute-start | bytes 1966088 | tf_op jit(solution)/shard_map/ppermute | solution.py:35
  77.6 3.2 %copy-start.4 = (bf16[1,128,4096]{2,1,0:T(8,128)(2,1)S(1)}, bf16[1,128,4096]{2,1,0:T(8,128)(2,1)}, u32[]{:S(2)}) copy-start(bf16[1,128,4096]{2,1,0:T(8,128)(2,1)} %param.7) | copy-start | bytes 3145732
  80.5 11.1 %collective-permute-start.30 = (bf16[384,512]{1,0:T(8,128)(2,1)S(1)}, bf16[384,512]{1,0:T(8,128)(2,1)S(1)}, u32[]{:S(2)}, u32[]{:S(2)}) collective-permute-start(bf16[384,512]{1,0:T(8,128)(2,1)S(1)} %project.2.refs_5_.refs_6_), channel_id=1, source_target_pairs={{0,2},{2,0},{1,3},{3,1},{4,6},{6,4},{5,7},{7,5},{8,10},{10,8},{9,1... | collective-permute-start | bytes 1179656 | tf_op jit(solution)/shard_map/ppermute | solution.py:35
  80.6 20.9 %collective-permute-start.28 = (bf16[384,512]{1,0:T(8,128)(2,1)S(1)}, bf16[384,512]{1,0:T(8,128)(2,1)S(1)}, u32[]{:S(2)}, u32[]{:S(2)}) collective-permute-start(bf16[384,512]{1,0:T(8,128)(2,1)S(1)} %project.2.refs_5_.refs_6_), channel_id=1, source_target_pairs={{0,1},{1,0},{2,3},{3,2},{4,5},{5,4},{6,7},{7,6},{8,9},{9,8},{10,11... | collective-permute-start | bytes 1179656 | tf_op jit(solution)/shard_map/ppermute | solution.py:35
  81.5 22.5 %copy-start.2 = (s32[1,16]{1,0:T(1,128)S(1)}, s32[1,16]{1,0:T(1,128)}, u32[]{:S(2)}) copy-start(s32[1,16]{1,0:T(1,128)} %refs_2_.5) | copy-start | bytes 196
  81.5 20.0 %collective-permute-start = (bf16[128,1024]{1,0:T(8,128)(2,1)S(1)}, bf16[128,1024]{1,0:T(8,128)(2,1)S(1)}, u32[]{:S(2)}, u32[]{:S(2)}) collective-permute-start(bf16[128,1024]{1,0:T(8,128)(2,1)S(1)} %get-tuple-element.55), channel_id=1, source_target_pairs={{0,8},{4,12},{8,0},{12,4},{1,9},{5,13},{9,1},{13,5},{2,10},{6,14},... | collective-permute-start | bytes 786440 | tf_op jit(solution)/shard_map/ppermute | solution.py:35
  91.7 12.4 %collective-permute-start.32 = (bf16[384,512]{1,0:T(8,128)(2,1)S(1)}, bf16[384,512]{1,0:T(8,128)(2,1)S(1)}, u32[]{:S(2)}, u32[]{:S(2)}) collective-permute-start(bf16[384,512]{1,0:T(8,128)(2,1)S(1)} %collective-permute-done.30.refs_9_.refs_10_), channel_id=1, source_target_pairs={{0,1},{1,0},{2,3},{3,2},{4,5},{5,4},{6,7},{7,6},{8,9},{9,8},{10,11... | collective-permute-start | bytes 1179656 | tf_op jit(solution)/shard_map/ppermute | solution.py:35
  97.6 5.1 %collective-permute-start.31 = (bf16[128,512]{1,0:T(8,128)(2,1)S(1)}, bf16[128,512]{1,0:T(8,128)(2,1)S(1)}, u32[]{:S(2)}, u32[]{:S(2)}) collective-permute-start(bf16[128,512]{1,0:T(8,128)(2,1)S(1)} %project.3.refs_6_.refs_7_), channel_id=1, source_target_pairs={{0,2},{2,0},{1,3},{3,1},{4,6},{6,4},{5,7},{7,5},{8,10},{10,8},{9,1... | collective-permute-start | bytes 393224 | tf_op jit(solution)/shard_map/ppermute | solution.py:35
  97.7 10.9 %collective-permute-start.34 = (bf16[128,1024]{1,0:T(8,128)(2,1)S(1)}, bf16[128,1024]{1,0:T(8,128)(2,1)S(1)}, u32[]{:S(2)}, u32[]{:S(2)}) collective-permute-start(bf16[128,1024]{1,0:T(8,128)(2,1)S(1)} %get-tuple-element.54), channel_id=1, source_target_pairs={{0,12},{4,0},{8,4},{12,8},{1,13},{5,1},{9,5},{13,9},{2,14},{6,2},{... | collective-permute-start | bytes 786440 | tf_op jit(solution)/shard_map/ppermute | solution.py:35
  101.5 8.6 %collective-permute-start.35 = (bf16[128,1024]{1,0:T(8,128)(2,1)S(1)}, bf16[128,1024]{1,0:T(8,128)(2,1)S(1)}, u32[]{:S(2)}, u32[]{:S(2)}) collective-permute-start(bf16[128,1024]{1,0:T(8,128)(2,1)S(1)} %get-tuple-element.53), channel_id=1, source_target_pairs={{0,4},{4,8},{8,12},{12,0},{1,5},{5,9},{9,13},{13,1},{2,6},{6,10},{... | collective-permute-start | bytes 786440 | tf_op jit(solution)/shard_map/ppermute | solution.py:35
  101.5 1.4 %collective-permute-start.29 = (bf16[128,512]{1,0:T(8,128)(2,1)S(1)}, bf16[128,512]{1,0:T(8,128)(2,1)S(1)}, u32[]{:S(2)}, u32[]{:S(2)}) collective-permute-start(bf16[128,512]{1,0:T(8,128)(2,1)S(1)} %project.3.refs_6_.refs_7_), channel_id=1, source_target_pairs={{0,1},{1,0},{2,3},{3,2},{4,5},{5,4},{6,7},{7,6},{8,9},{9,8},{10,11... | collective-permute-start | bytes 393224 | tf_op jit(solution)/shard_map/ppermute | solution.py:35
  102.7 1.3 collective-permute-start.33
  117.5 4.8 %collective-permute-start.39 = (f32[2,16,256]{2,1,0:T(8,128)S(1)}, f32[2,16,256]{2,1,0:T(8,128)S(1)}, u32[]{:S(2)}, u32[]{:S(2)}) collective-permute-start(f32[2,16,256]{2,1,0:T(8,128)S(1)} %dynamic-slice_bitcast_fusion), channel_id=1, source_target_pairs={{0,1},{1,0},{2,3},{3,2},{4,5},{5,4},{6,7},{7,6},{8,9},{9,8},{10,11... | collective-permute-start | bytes 98312 | tf_op jit(solution)/shard_map/ppermute | solution.py:35
  117.6 14.6 %collective-permute-start.36 = (bf16[128,1024]{1,0:T(8,128)(2,1)S(1)}, bf16[128,1024]{1,0:T(8,128)(2,1)S(1)}, u32[]{:S(2)}, u32[]{:S(2)}) collective-permute-start(bf16[128,1024]{1,0:T(8,128)(2,1)S(1)} %get-tuple-element.40), channel_id=1, source_target_pairs={{0,12},{4,0},{8,4},{12,8},{1,13},{5,1},{9,5},{13,9},{2,14},{6,2},{... | collective-permute-start | bytes 786440 | tf_op jit(solution)/shard_map/ppermute | solution.py:35
  120.8 14.8 %collective-permute-start.38 = (bf16[128,1024]{1,0:T(8,128)(2,1)S(1)}, bf16[128,1024]{1,0:T(8,128)(2,1)S(1)}, u32[]{:S(2)}, u32[]{:S(2)}) collective-permute-start(bf16[128,1024]{1,0:T(8,128)(2,1)S(1)} %get-tuple-element.42), channel_id=1, source_target_pairs={{0,4},{4,8},{8,12},{12,0},{1,5},{5,9},{9,13},{13,1},{2,6},{6,10},{... | collective-permute-start | bytes 786440 | tf_op jit(solution)/shard_map/ppermute | solution.py:35
  120.8 14.8 %collective-permute-start.37 = (bf16[128,1024]{1,0:T(8,128)(2,1)S(1)}, bf16[128,1024]{1,0:T(8,128)(2,1)S(1)}, u32[]{:S(2)}, u32[]{:S(2)}) collective-permute-start(bf16[128,1024]{1,0:T(8,128)(2,1)S(1)} %get-tuple-element.41), channel_id=1, source_target_pairs={{0,8},{4,12},{8,0},{12,4},{1,9},{5,13},{9,1},{13,5},{2,10},{6,14},... | collective-permute-start | bytes 786440 | tf_op jit(solution)/shard_map/ppermute | solution.py:35
  122.3 3.8 %collective-permute-start.40 = (f32[16,256]{1,0:T(8,128)S(1)}, f32[16,256]{1,0:T(8,128)S(1)}, u32[]{:S(2)}, u32[]{:S(2)}) collective-permute-start(f32[16,256]{1,0:T(8,128)S(1)} %dynamic-slice_bitcast_fusion.1), channel_id=1, source_target_pairs={{0,2},{2,0},{1,3},{3,1},{4,6},{6,4},{5,7},{7,5},{8,10},{10,8},{9,1... | collective-permute-start | bytes 49160 | tf_op jit(solution)/shard_map/ppermute | solution.py:35
